TPU v7x, 32 devices: a whole 2x2x4 slice. The times are simulated.
32 devices in a mesh: dp: 8 (over y, x, core), seq: 4 (over z).
Axes of the slice: x: 2, y: 2, z: 4, core: 2. Of those that a mesh axis runs over, the one named last changes fastest.
Arguments:
- tokens: bfloat16 [16, 1024, 768], P('dp', 'seq'), may hold values from -6 to 6
- chars: bfloat16 [16, 1024, 4, 768], P('dp', 'seq'), may hold values from -6 to 6
- char_counts: int32 [16, 1024], P('dp', 'seq'), may hold values from 1 to 4
- lengths: int32 [16], replicated, may hold values from 128 to 1024, as said below
- perm: int32 [2, 8], replicated, may hold values from 0 to 7, as said below
- token_out_cotangent: bfloat16 [16, 1024, 768], P('dp', 'seq'), may hold values from -6 to 6
- char_out_cotangent: bfloat16 [16, 1024, 768], P('dp', 'seq'), may hold values from -6 to 6
- w_qkv: float32 [768, 2304], P('dp'), may hold values from -0.21875 to 0.21875
- b_qv: float32 [1536], P('dp'), may hold values from -1.75 to 1.75
- w_out: float32 [768, 768], P('dp'), may hold values from -0.875 to 0.875
- w_in: float32 [768, 3072], P('dp'), may hold values from -0.21875 to 0.21875
- b_in: float32 [3072], P('dp'), may hold values from -1.75 to 1.75
- w_back: float32 [3072, 768], P('dp'), may hold values from -0.109375 to 0.109375
- gru_x: float32 [768, 2304], P('dp'), may hold values from -0.21875 to 0.21875
- gru_h: float32 [384, 2304], P('dp'), may hold values from -0.3125 to 0.3125
- gru_bias: float32 [2304, 2], P('dp'), may hold values from -1.75 to 1.75
- blend_w: float32 [768, 1536], P('dp'), may hold values from -0.21875 to 0.21875
- conv_w: float32 [4608, 1536], P('dp'), may hold values from -0.09375 to 0.09375
- conv_b: float32 [1536], P('dp'), may hold values from -1.75 to 1.75
- norm_gain: float32 [768, 4], P('dp'), may hold values from 0.1 to 1.9
- norm_bias: float32 [768, 4], P('dp'), may hold values from -1.75 to 1.75
- row_bias: float32 [768, 4], P('dp'), may hold values from -1.75 to 1.75
Outputs:
- token_out: bfloat16 [16, 1024, 768], P('dp', 'seq')
- char_out: bfloat16 [16, 1024, 768], P('dp', 'seq')
- tokens_grad: bfloat16 [16, 1024, 768], P('dp', 'seq')
- chars_grad: bfloat16 [16, 1024, 4, 768], P('dp', 'seq')
- w_qkv_grad: float32 [768, 2304], P('dp')
- b_qv_grad: float32 [1536], P('dp')
- w_out_grad: float32 [768, 768], P('dp')
- w_in_grad: float32 [768, 3072], P('dp')
- b_in_grad: float32 [3072], P('dp')
- w_back_grad: float32 [3072, 768], P('dp')
- gru_x_grad: float32 [768, 2304], P('dp')
- gru_h_grad: float32 [384, 2304], P('dp')
- gru_bias_grad: float32 [2304, 2], P('dp')
- blend_w_grad: float32 [768, 1536], P('dp')
- conv_w_grad: float32 [4608, 1536], P('dp')
- conv_b_grad: float32 [1536], P('dp')
- norm_gain_grad: float32 [768, 4], P('dp')
- norm_bias_grad: float32 [768, 4], P('dp')
- row_bias_grad: float32 [768, 4], P('dp')
Inputs may be any that keep to these rules, and one draw needn't show every extreme that they name: Positions j < lengths[s] of sequence s are valid keys; the first sequence is full and the second has exactly 128 valid positions. perm[m, g] is g xor perm[m, 0] (bitwise) for every group g; perm[m, 0] is never 0, and differs from one micro-batch to another. `char_counts`: characters of each token; its other rows of chars are unused.
All inputs are finite; a program needn't handle non-finite values.
Results may differ from a plain program's by a relative error of at most 0.019.
The roundings to bfloat16 on the way count: a program that leaves them out, or rounds other values in their place, can miss the bound.
Values may be sent and summed in bfloat16 or wider, within the bound.
A program may use at most 384 MiB of HBM per device.

v0:
```python
from functools import partial

import jax
import jax.numpy as jnp
from jax import lax
from jax.sharding import PartitionSpec as P

HEAD = 64
H = 384
NCHAR = 4


def partner(value, axis, apart):
    mask = 2**apart
    pairs = [(source, source ^ mask) for source in range(lax.axis_size(axis))]
    return lax.ppermute(value, axis, pairs)


def padded_2(block, sides, width):
    for axis, dim in sides:
        count = lax.axis_size(axis)
        forward = [(i, i + 1) for i in range(count - 1)]
        backward = [(target, source) for source, target in forward]
        low = lax.ppermute(
            lax.slice_in_dim(block, block.shape[dim] - width, None, axis=dim), axis, forward
        )
        high = lax.ppermute(lax.slice_in_dim(block, 0, width, axis=dim), axis, backward)
        block = jnp.concatenate([low, block, high], axis=dim)
    return block


def dot_plain(left, right):
    return jnp.dot(left, right, preferred_element_type=jnp.float32)


def dot_left(left, right):
    return lax.dot_general(
        left, right, (((0,), (0,)), ((), ())), preferred_element_type=jnp.float32
    )


def dot_right(left, right):
    return lax.dot_general(
        left, right, (((1,), (1,)), ((), ())), preferred_element_type=jnp.float32
    )


def column_sum(values):
    return jnp.sum(values.astype(jnp.float32), axis=0)


def norm_rows(values, gain, shift):
    center = values - jnp.mean(values, axis=-1, keepdims=True)
    spread = jnp.mean(center * center, axis=-1, keepdims=True)
    return center * lax.rsqrt(spread + 1e-06) * gain + shift


def norm_back(values, gain, shift, grad):
    result, pullback = jax.vjp(
        norm_rows, values, gain.astype(jnp.float32), shift.astype(jnp.float32)
    )
    return pullback(grad)


def gelu_exact(values):
    return jax.nn.gelu(values, approximate=False)


def gru_cell(live, gates, recur, state):
    width = state.shape[-1]
    reset = jax.nn.sigmoid(gates[:, :width] + recur[:, :width])
    update = jax.nn.sigmoid(gates[:, width : 2 * width] + recur[:, width : 2 * width])
    fresh = jnp.tanh(gates[:, 2 * width :] + reset * recur[:, 2 * width :])
    return jnp.where(live, (1.0 - update) * fresh + update * state, state)


def attention_scores(query, all_keys, valid):
    rows, width = query.shape
    heads = width // HEAD
    raw = jnp.einsum(
        "qhd,khd->hqk",
        query.reshape(rows, heads, HEAD),
        all_keys.reshape(-1, heads, HEAD),
        preferred_element_type=jnp.float32,
    )
    return jnp.where(valid[None, None, :], raw * HEAD ** (-0.5), -1e30)


def make_copies(masters):
    return [piece.astype(jnp.bfloat16) for piece in masters]


def fetch_shared(masters):
    copies = make_copies(masters)
    return (
        lax.all_gather(copies[0], "dp", axis=0, tiled=True),
        lax.all_gather(copies[1], "dp", axis=0, tiled=True),
        lax.all_gather(copies[2], "dp", axis=0, tiled=True),
        lax.all_gather(copies[3], "dp", axis=0, tiled=True),
        lax.all_gather(copies[4], "dp", axis=0, tiled=True),
        lax.all_gather(copies[5], "dp", axis=0, tiled=True),
        lax.all_gather(copies[6], "dp", axis=0, tiled=True),
        lax.all_gather(copies[7], "dp", axis=0, tiled=True),
        lax.all_gather(copies[8], "dp", axis=0, tiled=True),
        lax.all_gather(copies[9], "dp", axis=0, tiled=True),
        lax.all_gather(copies[10], "dp", axis=0, tiled=True),
        lax.all_gather(copies[11], "dp", axis=0, tiled=True),
        lax.all_gather(copies[12], "dp", axis=0, tiled=True),
        lax.all_gather(copies[13], "dp", axis=0, tiled=True),
        lax.all_gather(copies[14], "dp", axis=0, tiled=True),
    )


def relocate(mask, payload, returning):
    levels = lax.axis_size("dp").bit_length() - 1
    for bit in range(levels):
        moving = jnp.bitwise_and(mask, 1 << bit) != 0
        if returning:
            other = partner((payload[0], payload[1]), "dp", bit)
        else:
            other = partner((payload[0], payload[1], payload[2]), "dp", bit)
        payload = tuple((jnp.where(moving, fresh, older) for fresh, older in zip(other, payload)))
    return payload


def forward_pass(params, tokens_part, chars_part, counts_part, length_part):
    (
        w_qkv,
        b_qv,
        w_out,
        w_in,
        b_in,
        w_back,
        gru_x,
        gru_h,
        gru_bias,
        blend_w,
        conv_w,
        conv_b,
        norm_gain,
        norm_bias,
        row_bias,
    ) = params
    rows, width = tokens_part.shape
    heads = width // HEAD
    three = 3 * H
    padding = jnp.zeros((width,), jnp.bfloat16)
    project = dot_plain(tokens_part, w_qkv) + jnp.concatenate([b_qv[:width], padding, b_qv[width:]])
    query = project[:, :width].astype(jnp.bfloat16)
    keys = project[:, width : 2 * width].astype(jnp.bfloat16)
    values = project[:, 2 * width :].astype(jnp.bfloat16)
    all_keys, all_values = (
        lax.all_gather(keys, "seq", axis=0, tiled=True),
        lax.all_gather(values, "seq", axis=0, tiled=True),
    )
    valid = jnp.arange(all_keys.shape[0], dtype=jnp.int32) < length_part
    scores = attention_scores(query, all_keys, valid)
    top = jnp.max(scores, axis=-1, keepdims=True)
    log_total = top + jnp.log(jnp.sum(jnp.exp(scores - top), axis=-1, keepdims=True))
    shares = jnp.exp(scores - log_total).astype(jnp.bfloat16)
    context = (
        jnp.einsum(
            "hqk,khd->qhd",
            shares,
            all_values.reshape(-1, heads, HEAD),
            preferred_element_type=jnp.float32,
        )
        .reshape(rows, width)
        .astype(jnp.bfloat16)
    )
    summed_first = tokens_part.astype(jnp.float32) + dot_plain(context, w_out) + row_bias[:, 0]
    hidden1 = norm_rows(summed_first, norm_gain[:, 0], norm_bias[:, 0])
    hidden1_low = hidden1.astype(jnp.bfloat16)
    inner = dot_plain(hidden1_low, w_in) + b_in
    activated = gelu_exact(inner).astype(jnp.bfloat16)
    summed_second = hidden1 + dot_plain(activated, w_back) + row_bias[:, 1]
    hidden2 = norm_rows(summed_second, norm_gain[:, 1], norm_bias[:, 1])
    flat_chars = chars_part.reshape(rows * NCHAR, width)
    gates = (dot_plain(flat_chars, gru_x) + gru_bias[:, 0]).reshape(rows, NCHAR, 2 * three)
    ahead = [jnp.zeros((rows, H), jnp.float32)]
    ahead_low = []
    ahead_recur = []
    for position in range(NCHAR):
        live = (position < counts_part)[:, None]
        state_low = ahead[-1].astype(jnp.bfloat16)
        recur = dot_plain(state_low, gru_h[:, :three]) + gru_bias[:three, 1]
        ahead_low.append(state_low)
        ahead_recur.append(recur)
        ahead.append(gru_cell(live, gates[:, position, :three], recur, ahead[-1]))
    behind = [jnp.zeros((rows, H), jnp.float32)]
    behind_low = []
    behind_recur = []
    for order in range(NCHAR):
        position = NCHAR - 1 - order
        live = (position < counts_part)[:, None]
        state_low = behind[-1].astype(jnp.bfloat16)
        recur = dot_plain(state_low, gru_h[:, three:]) + gru_bias[three:, 1]
        behind_low.append(state_low)
        behind_recur.append(recur)
        behind.append(gru_cell(live, gates[:, position, three:], recur, behind[-1]))
    char_state = jnp.concatenate([ahead[-1], behind[-1]], axis=-1)
    hidden2_low = hidden2.astype(jnp.bfloat16)
    char_low = char_state.astype(jnp.bfloat16)
    token_side = dot_plain(hidden2_low, blend_w[:, :width]) + row_bias[:, 2]
    char_side = dot_plain(char_low, blend_w[:, width:]) + row_bias[:, 3]
    joined = jnp.concatenate([token_side, char_side], axis=-1).astype(jnp.bfloat16)
    padded = padded_2(joined, (("seq", 0),), 1)
    stacked = jnp.concatenate([padded[:-2], padded[1:-1], padded[2:]], axis=-1)
    mixed = dot_plain(stacked, conv_w) + conv_b
    lifted = gelu_exact(mixed)
    token_pre = hidden2 + lifted[:, :width]
    char_pre = char_state + lifted[:, width:]
    token_out = norm_rows(token_pre, norm_gain[:, 2], norm_bias[:, 2])
    char_out = norm_rows(char_pre, norm_gain[:, 3], norm_bias[:, 3])
    kept = {
        "query": query,
        "all_keys": all_keys,
        "all_values": all_values,
        "valid": valid,
        "log_total": log_total,
        "context": context,
        "summed_first": summed_first,
        "hidden1_low": hidden1_low,
        "inner": inner,
        "activated": activated,
        "summed_second": summed_second,
        "flat_chars": flat_chars,
        "gates": gates,
        "ahead": ahead,
        "ahead_low": ahead_low,
        "ahead_recur": ahead_recur,
        "behind": behind,
        "behind_low": behind_low,
        "behind_recur": behind_recur,
        "hidden2_low": hidden2_low,
        "char_low": char_low,
        "stacked": stacked,
        "mixed": mixed,
        "token_pre": token_pre,
        "char_pre": char_pre,
    }
    return (token_out, char_out, kept)


def backward_pass(params, kept, tokens_part, counts_part, token_cot, char_cot):
    (
        w_qkv,
        b_qv,
        w_out,
        w_in,
        b_in,
        w_back,
        gru_x,
        gru_h,
        gru_bias,
        blend_w,
        conv_w,
        conv_b,
        norm_gain,
        norm_bias,
        row_bias,
    ) = params
    rows, width = tokens_part.shape
    heads = width // HEAD
    three = 3 * H
    d_token_pre, gain_mix_token, shift_mix_token = norm_back(
        kept["token_pre"], norm_gain[:, 2], norm_bias[:, 2], token_cot.astype(jnp.float32)
    )
    d_char_pre, gain_mix_char, shift_mix_char = norm_back(
        kept["char_pre"], norm_gain[:, 3], norm_bias[:, 3], char_cot.astype(jnp.float32)
    )
    lift_value, lift_pull = jax.vjp(gelu_exact, kept["mixed"])
    d_mixed = lift_pull(jnp.concatenate([d_token_pre, d_char_pre], axis=-1))[0].astype(jnp.bfloat16)
    grad_conv = dot_left(kept["stacked"], d_mixed)
    grad_conv_bias = column_sum(d_mixed)
    beside_all = padded_2(d_mixed, (("seq", 0),), 1)
    shifted = jnp.concatenate([beside_all[2:], beside_all[1:-1], beside_all[:-2]], axis=-1).reshape(
        rows, 3, 2 * width
    )
    d_joined = jnp.einsum(
        "rto,tio->ri",
        shifted,
        conv_w.reshape(3, 2 * width, 2 * width),
        preferred_element_type=jnp.float32,
    ).astype(jnp.bfloat16)
    d_token_side = d_joined[:, :width]
    d_char_side = d_joined[:, width:]
    grad_blend = jnp.concatenate(
        [dot_left(kept["hidden2_low"], d_token_side), dot_left(kept["char_low"], d_char_side)],
        axis=-1,
    )
    d_hidden2 = d_token_pre + dot_right(d_token_side, blend_w[:, :width])
    d_char_state = d_char_pre + dot_right(d_char_side, blend_w[:, width:])
    gates = kept["gates"]
    d_ahead = d_char_state[:, :H]
    ahead_gates = [None] * NCHAR
    grad_ahead = jnp.zeros((H, three), jnp.float32)
    bias_ahead = jnp.zeros((three,), jnp.float32)
    for position in reversed(range(NCHAR)):
        live = (position < counts_part)[:, None]
        cell_value, cell_pull = jax.vjp(
            partial(gru_cell, live),
            gates[:, position, :three],
            kept["ahead_recur"][position],
            kept["ahead"][position],
        )
        d_gate, d_recur, d_state = cell_pull(d_ahead)
        d_recur = d_recur.astype(jnp.bfloat16)
        grad_ahead = grad_ahead + dot_left(kept["ahead_low"][position], d_recur)
        bias_ahead = bias_ahead + column_sum(d_recur)
        d_ahead = d_state + dot_right(d_recur, gru_h[:, :three])
        ahead_gates[position] = d_gate
    d_behind = d_char_state[:, H:]
    behind_gates = [None] * NCHAR
    grad_behind = jnp.zeros((H, three), jnp.float32)
    bias_behind = jnp.zeros((three,), jnp.float32)
    for order in reversed(range(NCHAR)):
        position = NCHAR - 1 - order
        live = (position < counts_part)[:, None]
        cell_value, cell_pull = jax.vjp(
            partial(gru_cell, live),
            gates[:, position, three:],
            kept["behind_recur"][order],
            kept["behind"][order],
        )
        d_gate, d_recur, d_state = cell_pull(d_behind)
        d_recur = d_recur.astype(jnp.bfloat16)
        grad_behind = grad_behind + dot_left(kept["behind_low"][order], d_recur)
        bias_behind = bias_behind + column_sum(d_recur)
        d_behind = d_state + dot_right(d_recur, gru_h[:, three:])
        behind_gates[position] = d_gate
    d_gates = jnp.stack(
        [
            jnp.concatenate([ahead_gates[position], behind_gates[position]], axis=-1)
            for position in range(NCHAR)
        ],
        axis=1,
    )
    d_gates = d_gates.astype(jnp.bfloat16).reshape(rows * NCHAR, 2 * three)
    grad_gru_x = dot_left(kept["flat_chars"], d_gates)
    grad_gru_bias = jnp.stack(
        [column_sum(d_gates), jnp.concatenate([bias_ahead, bias_behind])], axis=-1
    )
    chars_back = dot_right(d_gates, gru_x).reshape(rows, NCHAR, width).astype(jnp.bfloat16)
    d_second, gain_second, shift_second = norm_back(
        kept["summed_second"], norm_gain[:, 1], norm_bias[:, 1], d_hidden2
    )
    d_branch = d_second.astype(jnp.bfloat16)
    grad_back = dot_left(kept["activated"], d_branch)
    inner_value, inner_pull = jax.vjp(gelu_exact, kept["inner"])
    d_inner = inner_pull(dot_right(d_branch, w_back))[0].astype(jnp.bfloat16)
    grad_in = dot_left(kept["hidden1_low"], d_inner)
    d_hidden1 = d_second + dot_right(d_inner, w_in)
    d_first, gain_first, shift_first = norm_back(
        kept["summed_first"], norm_gain[:, 0], norm_bias[:, 0], d_hidden1
    )
    d_attend = d_first.astype(jnp.bfloat16)
    grad_out = dot_left(kept["context"], d_attend)
    d_context = dot_right(d_attend, w_out).astype(jnp.bfloat16)
    query = kept["query"]
    all_keys = kept["all_keys"]
    all_values = kept["all_values"]
    shares = jnp.exp(attention_scores(query, all_keys, kept["valid"]) - kept["log_total"])
    context_heads = d_context.reshape(rows, heads, HEAD)
    query_heads = query.reshape(rows, heads, HEAD)
    d_shares = jnp.einsum(
        "qhd,khd->hqk",
        context_heads,
        all_values.reshape(-1, heads, HEAD),
        preferred_element_type=jnp.float32,
    )
    delta = jnp.sum(d_shares * shares, axis=-1, keepdims=True)
    d_scores = (shares * (d_shares - delta)).astype(jnp.bfloat16)
    shares_low = shares.astype(jnp.bfloat16)
    scale = HEAD ** (-0.5)
    d_query = (
        jnp.einsum(
            "hqk,khd->qhd",
            d_scores,
            all_keys.reshape(-1, heads, HEAD),
            preferred_element_type=jnp.float32,
        )
        * scale
    ).reshape(rows, width)
    count = rows * lax.axis_size("seq")
    d_key = (
        jnp.einsum("hqk,qhd->khd", d_scores, query_heads, preferred_element_type=jnp.float32)
        * scale
    )
    d_value = jnp.einsum(
        "hqk,qhd->khd", shares_low, context_heads, preferred_element_type=jnp.float32
    )
    key_grads = lax.psum_scatter(
        jnp.concatenate(
            [d_key.reshape(count, width), d_value.reshape(count, width)], axis=-1
        ).astype(jnp.bfloat16),
        "seq",
        scatter_dimension=0,
        tiled=True,
    ).astype(jnp.float32)
    d_project = jnp.concatenate([d_query, key_grads], axis=-1).astype(jnp.bfloat16)
    grad_qkv = dot_left(tokens_part, d_project)
    project_sums = column_sum(d_project)
    grad_b_qv = jnp.concatenate([project_sums[:width], project_sums[2 * width :]])
    tokens_back = (d_first + dot_right(d_project, w_qkv)).astype(jnp.bfloat16)
    grad_gain = jnp.stack([gain_first, gain_second, gain_mix_token, gain_mix_char], axis=-1)
    grad_shift = jnp.stack([shift_first, shift_second, shift_mix_token, shift_mix_char], axis=-1)
    grad_rows = jnp.stack(
        [
            column_sum(d_attend),
            column_sum(d_branch),
            column_sum(d_token_side),
            column_sum(d_char_side),
        ],
        axis=-1,
    )
    grads = (
        grad_qkv,
        grad_b_qv,
        grad_out,
        grad_in,
        column_sum(d_inner),
        grad_back,
        grad_gru_x,
        jnp.concatenate([grad_ahead, grad_behind], axis=-1),
        grad_gru_bias,
        grad_blend,
        grad_conv,
        grad_conv_bias,
        grad_gain,
        grad_shift,
        grad_rows,
    )
    return (tokens_back, chars_back, grads)


def body(
    tokens,
    chars,
    char_counts,
    lengths,
    perm,
    token_out_cotangent,
    char_out_cotangent,
    w_qkv,
    b_qv,
    w_out,
    w_in,
    b_in,
    w_back,
    gru_x,
    gru_h,
    gru_bias,
    blend_w,
    conv_w,
    conv_b,
    norm_gain,
    norm_bias,
    row_bias,
):
    masters = (
        w_qkv,
        b_qv,
        w_out,
        w_in,
        b_in,
        w_back,
        gru_x,
        gru_h,
        gru_bias,
        blend_w,
        conv_w,
        conv_b,
        norm_gain,
        norm_bias,
        row_bias,
    )
    shared = fetch_shared(masters)
    micro = tokens.shape[0]
    place = lax.axis_index("dp")
    token_rows = []
    char_rows = []
    token_backs = []
    char_backs = []
    totals = ()
    for batch in range(micro):
        mask = perm[batch, 0]
        moved = relocate(
            mask, (tokens[batch], chars[batch], char_counts[batch].astype(jnp.bfloat16)), False
        )
        tokens_here = moved[0]
        chars_here = moved[1]
        counts_here = moved[2].astype(jnp.int32)
        length_here = lengths[jnp.bitwise_xor(place, mask) * micro + batch]
        params = shared
        token_out, char_out, kept = forward_pass(
            params, tokens_here, chars_here, counts_here, length_here
        )
        params = shared
        tokens_back, chars_back, grads = backward_pass(
            params,
            kept,
            tokens_here,
            counts_here,
            token_out_cotangent[batch],
            char_out_cotangent[batch],
        )
        returned = relocate(mask, (tokens_back, chars_back), True)
        token_rows.append(token_out.astype(jnp.bfloat16))
        char_rows.append(char_out.astype(jnp.bfloat16))
        token_backs.append(returned[0])
        char_backs.append(returned[1])
        totals = (
            grads if batch == 0 else tuple((left + right for left, right in zip(totals, grads)))
        )
    devices_all = lax.axis_size("dp") * lax.axis_size("seq")
    flat = tuple((total.reshape(devices_all, -1) for total in totals))
    shards = (
        lax.psum_scatter(flat[0], ("dp", "seq"), scatter_dimension=0, tiled=True),
        lax.psum_scatter(flat[1], ("dp", "seq"), scatter_dimension=0, tiled=True),
        lax.psum_scatter(flat[2], ("dp", "seq"), scatter_dimension=0, tiled=True),
        lax.psum_scatter(flat[3], ("dp", "seq"), scatter_dimension=0, tiled=True),
        lax.psum_scatter(flat[4], ("dp", "seq"), scatter_dimension=0, tiled=True),
        lax.psum_scatter(flat[5], ("dp", "seq"), scatter_dimension=0, tiled=True),
        lax.psum_scatter(flat[6], ("dp", "seq"), scatter_dimension=0, tiled=True),
        lax.psum_scatter(flat[7], ("dp", "seq"), scatter_dimension=0, tiled=True),
        lax.psum_scatter(flat[8], ("dp", "seq"), scatter_dimension=0, tiled=True),
        lax.psum_scatter(flat[9], ("dp", "seq"), scatter_dimension=0, tiled=True),
        lax.psum_scatter(flat[10], ("dp", "seq"), scatter_dimension=0, tiled=True),
        lax.psum_scatter(flat[11], ("dp", "seq"), scatter_dimension=0, tiled=True),
        lax.psum_scatter(flat[12], ("dp", "seq"), scatter_dimension=0, tiled=True),
        lax.psum_scatter(flat[13], ("dp", "seq"), scatter_dimension=0, tiled=True),
        lax.psum_scatter(flat[14], ("dp", "seq"), scatter_dimension=0, tiled=True),
    )
    pieces = (
        lax.all_gather(shards[0].astype(jnp.bfloat16), "seq", axis=0, tiled=True).astype(
            jnp.float32
        ),
        lax.all_gather(shards[1].astype(jnp.bfloat16), "seq", axis=0, tiled=True).astype(
            jnp.float32
        ),
        lax.all_gather(shards[2].astype(jnp.bfloat16), "seq", axis=0, tiled=True).astype(
            jnp.float32
        ),
        lax.all_gather(shards[3].astype(jnp.bfloat16), "seq", axis=0, tiled=True).astype(
            jnp.float32
        ),
        lax.all_gather(shards[4].astype(jnp.bfloat16), "seq", axis=0, tiled=True).astype(
            jnp.float32
        ),
        lax.all_gather(shards[5].astype(jnp.bfloat16), "seq", axis=0, tiled=True).astype(
            jnp.float32
        ),
        lax.all_gather(shards[6].astype(jnp.bfloat16), "seq", axis=0, tiled=True).astype(
            jnp.float32
        ),
        lax.all_gather(shards[7].astype(jnp.bfloat16), "seq", axis=0, tiled=True).astype(
            jnp.float32
        ),
        lax.all_gather(shards[8].astype(jnp.bfloat16), "seq", axis=0, tiled=True).astype(
            jnp.float32
        ),
        lax.all_gather(shards[9].astype(jnp.bfloat16), "seq", axis=0, tiled=True).astype(
            jnp.float32
        ),
        lax.all_gather(shards[10].astype(jnp.bfloat16), "seq", axis=0, tiled=True).astype(
            jnp.float32
        ),
        lax.all_gather(shards[11].astype(jnp.bfloat16), "seq", axis=0, tiled=True).astype(
            jnp.float32
        ),
        lax.all_gather(shards[12].astype(jnp.bfloat16), "seq", axis=0, tiled=True).astype(
            jnp.float32
        ),
        lax.all_gather(shards[13].astype(jnp.bfloat16), "seq", axis=0, tiled=True).astype(
            jnp.float32
        ),
        lax.all_gather(shards[14].astype(jnp.bfloat16), "seq", axis=0, tiled=True).astype(
            jnp.float32
        ),
    )
    summed = [piece.reshape(master.shape) for piece, master in zip(pieces, masters)]
    return (
        jnp.stack(token_rows),
        jnp.stack(char_rows),
        jnp.stack(token_backs),
        jnp.stack(char_backs),
        summed[0],
        summed[1],
        summed[2],
        summed[3],
        summed[4],
        summed[5],
        summed[6],
        summed[7],
        summed[8],
        summed[9],
        summed[10],
        summed[11],
        summed[12],
        summed[13],
        summed[14],
    )


def solution(mesh):
    return jax.shard_map(
        body,
        mesh=mesh,
        in_specs=(
            P("dp", "seq", None),
            P("dp", "seq", None, None),
            P("dp", "seq"),
            P(),
            P(),
            P("dp", "seq", None),
            P("dp", "seq", None),
            P("dp", None),
            P("dp"),
            P("dp", None),
            P("dp", None),
            P("dp"),
            P("dp", None),
            P("dp", None),
            P("dp", None),
            P("dp", None),
            P("dp", None),
            P("dp", None),
            P("dp"),
            P("dp", None),
            P("dp", None),
            P("dp", None),
        ),
        out_specs=(
            P("dp", "seq", None),
            P("dp", "seq", None),
            P("dp", "seq", None),
            P("dp", "seq", None, None),
            P("dp", None),
            P("dp"),
            P("dp", None),
            P("dp", None),
            P("dp"),
            P("dp", None),
            P("dp", None),
            P("dp", None),
            P("dp", None),
            P("dp", None),
            P("dp", None),
            P("dp"),
            P("dp", None),
            P("dp", None),
            P("dp", None),
        ),
        check_vma=False,
    )
```

profile of v0, /device:TPU:0, one launch (start us, length us, event | category | flops | bytes accessed | tf_op | source)
XLA Modules:
  0.0 2567.2 jit_solution(1331552772848401342)
XLA Ops:
  18.2 12.8 collective-permute-done.12
  35.9 12.9 all-reduce.82
  176.6 60.6 %collective-permute-done.4 = bf16[256]{0:T(256)(128)(2,1)S(1)} collective-permute-done((bf16[256]{0:T(256)(128)(2,1)S(1)}, bf16[256]{0:T(256)(128)(2,1)S(1)}, u32[]{:S(2)}, u32[]{:S(2)}) %collective-permute-start.4) | collective-permute-done | bytes 544 | tf_op jit(solution)/shard_map/ppermute | solution.py:16
  250.9 28.7 %collective-permute-done.19 = bf16[256,4,768]{2,0,1:T(8,128)(2,1)} collective-permute-done((bf16[256,4,768]{2,0,1:T(8,128)(2,1)}, bf16[256,4,768]{2,0,1:T(8,128)(2,1)}, u32[]{:S(2)}, u32[]{:S(2)}) %collective-permute-start.19) | collective-permute-done | bytes 1572896 | tf_op jit(solution)/shard_map/ppermute | solution.py:16
  288.5 22.7 collective-permute-done.8
  344.2 18.1 fusion.621
  390.1 18.1 fusion.622
  495.5 11.9 multiply_convert_fusion.5
  541.0 12.0 multiply_multiply_fusion.21
  553.1 12.1 multiply_multiply_fusion.20
  595.6 13.2 fusion.543
  608.8 22.5 convolution_add_fusion
  631.3 28.7 %reshape.773 = f32[32,221184]{1,0:T(8,128)} reshape(f32[4608,1536]{1,0:T(8,128)} %convolution_add_fusion) | data formatting | bytes 56623104 | tf_op jit(solution)/shard_map/reshape | solution.py:517
  965.7 26.7 %collective-permute-done.33 = bf16[256,4,768]{2,0,1:T(8,128)(2,1)S(1)} collective-permute-done((bf16[256,4,768]{2,0,1:T(8,128)(2,1)S(1)}, bf16[256,4,768]{2,0,1:T(8,128)(2,1)S(1)}, u32[]{:S(2)}, u32[]{:S(2)}) %collective-permute-start.33) | collective-permute-done | bytes 1572896 | tf_op jit(solution)/shard_map/ppermute | solution.py:16
  994.9 30.2 %collective-permute-done.36 = bf16[256,4,768]{2,0,1:T(8,128)(2,1)S(1)} collective-permute-done((bf16[256,4,768]{2,0,1:T(8,128)(2,1)S(1)}, bf16[256,4,768]{2,0,1:T(8,128)(2,1)S(1)}, u32[]{:S(2)}, u32[]{:S(2)}) %collective-permute-start.36) | collective-permute-done | bytes 1572896 | tf_op jit(solution)/shard_map/ppermute | solution.py:16
  1093.8 1146.3 %all-reduce.84 = (bf16[32,55296]{1,0:T(8,128)(2,1)}, bf16[32,48]{1,0:T(8,128)(2,1)}, bf16[32,18432]{1,0:T(8,128)(2,1)}, bf16[32,73728]{1,0:T(8,128)(2,1)}, bf16[...) all-reduce(f32[32,55296]{1,0:T(8,128)} %reshape.748, ...), channel_id=4, replica_groups=mesh['dp'=8,'seq'=4] {'dp','seq'}, use_global_device_ids=true, to_apply=%region_40.41.clone | all-reduce | flops 18009600 | bytes 108057600
  2310.6 14.1 all-gather.7
  2334.1 18.2 all-gather.12
  2353.6 23.3 all-gather.14
  2378.7 32.4 %all-gather.11 = bf16[4,1,55296]{2,1,0:T(2,128)(2,1)S(1)} all-gather(bf16[1,1,55296]{2,1,0:T(2,128)(2,1)S(1)} %fusion.380), channel_id=1, replica_groups=mesh['dp'=8,'seq'=4] {'seq'}, dimensions={0}, use_global_device_ids=true | all-gather | bytes 552960 | tf_op jit(solution)/shard_map/all_gather | solution.py:554
  2413.8 26.5 %all-gather.5 = bf16[4,1,55296]{2,1,0:T(2,128)(2,1)S(1)} all-gather(bf16[1,1,55296]{2,1,0:T(2,128)(2,1)S(1)} %fusion.381), channel_id=1, replica_groups=mesh['dp'=8,'seq'=4] {'seq'}, dimensions={0}, use_global_device_ids=true | all-gather | bytes 552960 | tf_op jit(solution)/shard_map/all_gather | solution.py:536
  2453.9 24.0 all-gather.10
  2487.6 17.0 all-gather.8
  2517.7 38.5 %convert_reduce_fusion.2 = f32[4,221184]{1,0:T(4,128)S(1)} fusion(bf16[4,1,221184]{2,1,0:T(2,128)(2,1)} %all-gather.58.cloned.1.call-done), kind=kLoop, calls=%fused_computation.39 | loop fusion | flops 884736 | bytes 5308416 | tf_op jit(solution)/shard_map/reshape | solution.py:582
  (1477 shorter events, 870.6 us)
Async XLA Ops:
  9.4 238.3 %all-gather.50.cloned.1.call-start = ((), (), s32[]{:S(2)}) async-start(), calls=%async_computation.10 | async-start | bytes 1990656 | tf_op jit(solution)/shard_map/all_gather | solution.py:103
  10.2 312.7 %all-gather.48.cloned.1.call-start = ((), (), s32[]{:S(2)}) async-start(), calls=%async_computation.9 | async-start | bytes 3981312 | tf_op jit(solution)/shard_map/all_gather | solution.py:102
  11.1 425.9 %all-gather.46.cloned.1.call-start = ((), (), s32[]{:S(2)}) async-start(), calls=%async_computation.8 | async-start | bytes 2654208 | tf_op jit(solution)/shard_map/all_gather | solution.py:105
  11.9 446.4 %all-gather.56.cloned.1.call-start = ((), (), s32[]{:S(2)}) async-start(), calls=%async_computation.13 | async-start | bytes 1966080 | tf_op jit(solution)/shard_map/all_gather | solution.py:153
  56.2 404.0 %all-gather.54.cloned.1.call-start = ((), (), s32[]{:S(2)}) async-start(), calls=%async_computation.12 | async-start | bytes 1966080 | tf_op jit(solution)/shard_map/all_gather | solution.py:154
  56.8 406.5 %all-gather.38.cloned.1.call-start = ((), (), s32[]{:S(2)}) async-start(), calls=%async_computation.4 | async-start | bytes 1966080 | tf_op jit(solution)/shard_map/all_gather | solution.py:153
  89.3 375.7 %all-gather.36.cloned.1.call-start = ((), (), s32[]{:S(2)}) async-start(), calls=%async_computation.3 | async-start | bytes 1966080 | tf_op jit(solution)/shard_map/all_gather | solution.py:154
  90.1 394.9 %all-gather.40.cloned.1.call-start = ((), (), s32[]{:S(2)}) async-start(), calls=%async_computation.5 | async-start | bytes 1327104 | tf_op jit(solution)/shard_map/all_gather | solution.py:98
  90.8 404.7 %all-gather.42.cloned.1.call-start = ((), (), s32[]{:S(2)}) async-start(), calls=%async_computation.6 | async-start | bytes 5308416 | tf_op jit(solution)/shard_map/all_gather | solution.py:99
  91.8 415.6 %all-gather.44.cloned.1.call-start = ((), (), s32[]{:S(2)}) async-start(), calls=%async_computation.7 | async-start | bytes 5308416 | tf_op jit(solution)/shard_map/all_gather | solution.py:101
  92.8 447.7 %all-gather.52.cloned.1.call-start = ((), (), s32[]{:S(2)}) async-start(), calls=%async_computation.11 | async-start | bytes 15925248 | tf_op jit(solution)/shard_map/all_gather | solution.py:106
  93.4 79.9 %collective-permute-start.3 = (bf16[256]{0:T(256)(128)(2,1)}, bf16[256]{0:T(256)(128)(2,1)}, u32[]{:S(2)}, u32[]{:S(2)}) collective-permute-start(bf16[256]{0:T(256)(128)(2,1)} %get-tuple-element.122), channel_id=1, source_target_pairs={{0,4},{4,0},{8,12},{12,8},{16,20},{20,16},{24,28},{28,24},{1,5},{5... | collective-permute-start | bytes 1544 | tf_op jit(solution)/shard_map/ppermute | solution.py:16
  93.4 82.0 %collective-permute-start.14 = (bf16[256]{0:T(256)(128)(2,1)}, bf16[256]{0:T(256)(128)(2,1)}, u32[]{:S(2)}, u32[]{:S(2)}) collective-permute-start(bf16[256]{0:T(256)(128)(2,1)} %get-tuple-element.123), channel_id=1, source_target_pairs={{0,4},{4,0},{8,12},{12,8},{16,20},{20,16},{24,28},{28,24},{1,5},{5... | collective-permute-start | bytes 1544 | tf_op jit(solution)/shard_map/ppermute | solution.py:16
  101.5 966.8 %reduce-scatter.5.cloned.1.call-start = ((), (), s32[]{:S(2)}) async-start(), calls=%async_computation.15 | async-start | bytes 3932160 | tf_op jit(solution)/shard_map/reduce_scatter | solution.py:393
  166.5 72.8 %collective-permute-start.18 = (bf16[256,4,768]{2,0,1:T(8,128)(2,1)}, bf16[256,4,768]{2,0,1:T(8,128)(2,1)}, u32[]{:S(2)}, u32[]{:S(2)}) collective-permute-start(bf16[256,4,768]{2,0,1:T(8,128)(2,1)} %broadcast_select_fusion.1), channel_id=1, source_target_pairs={{0,8},{4,12},{8,0},{12,4},{16,24},{20,28},{24,16},{28,20},{1,9},{5... | collective-permute-start | bytes 4718600 | tf_op jit(solution)/shard_map/ppermute | solution.py:16
  168.3 75.2 %collective-permute-start.7 = (bf16[256,4,768]{2,0,1:T(8,128)(2,1)S(1)}, bf16[256,4,768]{2,0,1:T(8,128)(2,1)S(1)}, u32[]{:S(2)}, u32[]{:S(2)}) collective-permute-start(bf16[256,4,768]{2,0,1:T(8,128)(2,1)S(1)} %broadcast_select_fusion.6), channel_id=1, source_target_pairs={{0,8},{4,12},{8,0},{12,4},{16,24},{20,28},{24,16},{28,20},{1,9},{5... | collective-permute-start | bytes 4718600 | tf_op jit(solution)/shard_map/ppermute | solution.py:16
  579.1 102.5 %collective-permute-start.27 = (bf16[1,1536]{1,0:T(2,128)(2,1)}, bf16[1,1536]{1,0:T(2,128)(2,1)S(1)}, u32[]{:S(2)}, u32[]{:S(2)}) collective-permute-start(bf16[1,1536]{1,0:T(2,128)(2,1)} %get-tuple-element.393), channel_id=1, source_target_pairs={{1,0},{2,1},{3,2},{5,4},{6,5},{7,6},{9,8},{10,9},{11,10},{13,12},{... | collective-permute-start | bytes 9224 | tf_op jit(solution)/shard_map/ppermute | solution.py:27
  580.4 101.2 %collective-permute-start.28 = (bf16[1,1536]{1,0:T(2,128)(2,1)}, bf16[1,1536]{1,0:T(2,128)(2,1)}, u32[]{:S(2)}, u32[]{:S(2)}) collective-permute-start(bf16[1,1536]{1,0:T(2,128)(2,1)} %get-tuple-element.394), channel_id=1, source_target_pairs={{0,1},{1,2},{2,3},{4,5},{5,6},{6,7},{8,9},{9,10},{10,11},{12,13},{... | collective-permute-start | bytes 9224 | tf_op jit(solution)/shard_map/ppermute | solution.py:24
  586.1 73.9 %collective-permute-start.22 = (bf16[1,1536]{1,0:T(2,128)(2,1)}, bf16[1,1536]{1,0:T(2,128)(2,1)}, u32[]{:S(2)}, u32[]{:S(2)}) collective-permute-start(bf16[1,1536]{1,0:T(2,128)(2,1)} %get-tuple-element.391), channel_id=1, source_target_pairs={{1,0},{2,1},{3,2},{5,4},{6,5},{7,6},{9,8},{10,9},{11,10},{13,12},{... | collective-permute-start | bytes 9224 | tf_op jit(solution)/shard_map/ppermute | solution.py:27
  587.4 72.6 %collective-permute-start.23 = (bf16[1,1536]{1,0:T(2,128)(2,1)}, bf16[1,1536]{1,0:T(2,128)(2,1)}, u32[]{:S(2)}, u32[]{:S(2)}) collective-permute-start(bf16[1,1536]{1,0:T(2,128)(2,1)} %get-tuple-element.392), channel_id=1, source_target_pairs={{0,1},{1,2},{2,3},{4,5},{5,6},{6,7},{8,9},{9,10},{10,11},{12,13},{... | collective-permute-start | bytes 9224 | tf_op jit(solution)/shard_map/ppermute | solution.py:24
  893.2 181.0 %reduce-scatter.3.cloned.1.call-start = ((), (), s32[]{:S(2)}) async-start(), calls=%async_computation.14 | async-start | bytes 3932160 | tf_op jit(solution)/shard_map/reduce_scatter | solution.py:393
  944.3 1573.3 %all-gather.58.cloned.1.call-start = ((), (), s32[]{:S(2)}) async-start(), calls=%async_computation.16 | async-start | bytes 4423680 | tf_op jit(solution)/shard_map/all_gather | solution.py:566
  1074.2 1409.1 %collective-permute-start.29 = (bf16[256,768]{1,0:T(8,128)(2,1)}, bf16[256,768]{1,0:T(8,128)(2,1)}, u32[]{:S(2)}, u32[]{:S(2)}) collective-permute-start(bf16[256,768]{1,0:T(8,128)(2,1)} %fusion.55), channel_id=1, source_target_pairs={{0,4},{4,0},{8,12},{12,8},{16,20},{20,16},{24,28},{28,24},{1,5},{5... | collective-permute-start | bytes 1179656 | tf_op jit(solution)/shard_map/ppermute | solution.py:16
  1093.2 1392.8 %collective-permute-start.24 = (bf16[256,768]{1,0:T(8,128)(2,1)}, bf16[256,768]{1,0:T(8,128)(2,1)}, u32[]{:S(2)}, u32[]{:S(2)}) collective-permute-start(bf16[256,768]{1,0:T(8,128)(2,1)} %fusion.54), channel_id=1, source_target_pairs={{0,4},{4,0},{8,12},{12,8},{16,20},{20,16},{24,28},{28,24},{1,5},{5... | collective-permute-start | bytes 1179656 | tf_op jit(solution)/shard_map/ppermute | solution.py:16
  (470 other events, 3129.3 us)
Sparse Core Ops, SparseCore 0:
  10.5 41.5 all-gather.33
  54.6 32.9 all-gather.49
  90.0 35.5 all-gather.47
  128.0 28.8 all-gather.45
  158.9 37.0 all-gather.55
  197.9 35.8 all-gather.53
  236.0 35.8 all-gather.37
  273.5 35.8 all-gather.35
  311.3 22.7 all-gather.39
  336.4 38.7 all-gather.41
  377.7 38.7 all-gather.43
  418.3 78.6 all-gather.51
  893.3 58.7 reduce-scatter.4
  954.9 60.3 reduce-scatter.2
  2334.3 101.8 all-gather.57
where the time goes:
time: 2580 us; the launch traced here: 2570 us
  blocking collectives  1420 us (55%)
  local copies, waits for them, and re-layouts  323 us (13%)
  matrix products  314 us (12%)
  waiting for transfers between devices  218 us (8%)
  other arithmetic  211 us (8%)
  starting transfers between devices  56 us (2%)
    unnamed x2, blocking collectives  1160 us
    ppermute x30, waiting for transfers between devices, partner(): return lax.ppermute(value, axis, pairs)  213 us
    unnamed x930, local copies, waits for them, and re-layouts  107 us
    dot_general x32, matrix products, dot_left(): lax.dot_general(left, right, (((0,), (0,)), ((), ())), preferred_element_...  101 us
    dot_general x30, matrix products, dot_plain(): return jnp.dot(left, right, preferred_element_type=jnp.float32)  92.6 us
    reshape x6, local copies, waits for them, and re-layouts, body(): flat = tuple((total.reshape(devices_all, -1) for total in totals))  60.5 us
    reshape x15, other arithmetic, body(): piece.reshape(master.shape)  55.1 us
  transfers between devices with their start and end apart: 53, of which 12 were waited for; matrix products, arithmetic and copies ran while one was open for 21% of the time, Pallas kernels for 0%

commit v1 on v0

v1 whole, which is shorter than its diff:
```python
from functools import partial

import jax
import jax.numpy as jnp
from jax import lax
from jax.experimental import pallas as pl
from jax.experimental.pallas import tpu as pltpu
from jax.sharding import PartitionSpec as P

HEAD = 64
H = 384
NCHAR = 4
WIDE = 768
BF = jnp.bfloat16
F32 = jnp.float32


def dot_plain(left, right):
    return jnp.dot(left, right, preferred_element_type=F32)


def dot_left(left, right):
    return lax.dot_general(left, right, (((0,), (0,)), ((), ())), preferred_element_type=F32)


def dot_right(left, right):
    return lax.dot_general(left, right, (((1,), (1,)), ((), ())), preferred_element_type=F32)


def column_sum(values):
    return jnp.sum(values.astype(F32), axis=0)


def norm_rows(values, gain, shift):
    center = values - jnp.mean(values, axis=-1, keepdims=True)
    spread = jnp.mean(center * center, axis=-1, keepdims=True)
    rstd = lax.rsqrt(spread + 1e-06)
    return center * rstd * gain + shift


def norm_back(values, gain, grad):
    center = values - jnp.mean(values, axis=-1, keepdims=True)
    spread = jnp.mean(center * center, axis=-1, keepdims=True)
    rstd = lax.rsqrt(spread + 1e-06)
    hat = center * rstd
    lead = grad * gain
    back = rstd * (
        lead
        - jnp.mean(lead, axis=-1, keepdims=True)
        - hat * jnp.mean(lead * hat, axis=-1, keepdims=True)
    )
    return back, jnp.sum(grad * hat, axis=0), jnp.sum(grad, axis=0)


def gelu_exact(values):
    return jax.nn.gelu(values, approximate=False)


def gelu_slope(values):
    cdf = 0.5 * (1.0 + lax.erf(values * (0.5**0.5)))
    pdf = jnp.exp(-0.5 * values * values) * 0.3989422804014327
    return cdf + values * pdf


def gru_cell(live, gates, recur, state):
    width = state.shape[-1]
    reset = jax.nn.sigmoid(gates[:, :width] + recur[:, :width])
    update = jax.nn.sigmoid(gates[:, width : 2 * width] + recur[:, width : 2 * width])
    fresh = jnp.tanh(gates[:, 2 * width :] + reset * recur[:, 2 * width :])
    return jnp.where(live, (1.0 - update) * fresh + update * state, state)


def attention_forward_kernel(per, len_ref, qkv_ref, out_ref):
    block = pl.program_id(1)
    length = len_ref[pl.program_id(0)]
    span = per * HEAD
    total = qkv_ref.shape[0] * qkv_ref.shape[2]
    rows = qkv_ref.shape[2]
    q_all = qkv_ref[block, 0, :, :span]
    k_all = qkv_ref[:, 0, :, span : 2 * span].reshape(total, span)
    v_all = qkv_ref[:, 0, :, 2 * span :].reshape(total, span)
    valid = lax.broadcasted_iota(jnp.int32, (rows, total), 1) < length
    pieces = []
    for j in range(per):
        part = slice(j * HEAD, (j + 1) * HEAD)
        scores = dot_right(q_all[:, part], k_all[:, part]) * HEAD ** (-0.5)
        scores = jnp.where(valid, scores, -1e30)
        raised = jnp.exp(scores - jnp.max(scores, axis=-1, keepdims=True))
        probs = (raised / jnp.sum(raised, axis=-1, keepdims=True)).astype(BF)
        pieces.append(dot_plain(probs, v_all[:, part]))
    out_ref[0, 0] = jnp.concatenate(pieces, axis=-1).astype(BF)


def attention_forward(qkv, lengths, per):
    seqs, rows = qkv.shape[1], qkv.shape[2]
    parts = qkv.shape[0]
    span = per * HEAD
    return pl.pallas_call(
        partial(attention_forward_kernel, per),
        grid_spec=pltpu.PrefetchScalarGridSpec(
            num_scalar_prefetch=1,
            grid=(seqs, parts),
            in_specs=[pl.BlockSpec((parts, 1, rows, 3 * span), lambda m, b, n: (0, m, 0, 0))],
            out_specs=pl.BlockSpec((1, 1, rows, span), lambda m, b, n: (b, m, 0, 0)),
        ),
        out_shape=jax.ShapeDtypeStruct((parts, seqs, rows, span), BF),
        name="attend_forward",
    )(lengths, qkv)


def attention_backward_kernel(per, len_ref, qkv_ref, grad_ref, out_ref, key_acc, value_acc):
    block = pl.program_id(1)
    length = len_ref[pl.program_id(0)]
    span = per * HEAD
    parts, rows = qkv_ref.shape[0], qkv_ref.shape[2]
    total = parts * rows
    scale = HEAD ** (-0.5)

    @pl.when(block == 0)
    def _():
        key_acc[...] = jnp.zeros_like(key_acc)
        value_acc[...] = jnp.zeros_like(value_acc)

    q_all = qkv_ref[block, 0, :, :span]
    g_all = grad_ref[block, 0]
    k_all = qkv_ref[:, 0, :, span : 2 * span].reshape(total, span)
    v_all = qkv_ref[:, 0, :, 2 * span :].reshape(total, span)
    valid = lax.broadcasted_iota(jnp.int32, (total, rows), 0) < length
    q_pieces, k_pieces, v_pieces = [], [], []
    for j in range(per):
        part = slice(j * HEAD, (j + 1) * HEAD)
        q, g, k, v = q_all[:, part], g_all[:, part], k_all[:, part], v_all[:, part]
        scores = jnp.where(valid, dot_right(k, q) * scale, -1e30)
        raised = jnp.exp(scores - jnp.max(scores, axis=0, keepdims=True))
        probs = raised / jnp.sum(raised, axis=0, keepdims=True)
        d_probs = dot_right(v, g)
        delta = jnp.sum(d_probs * probs, axis=0, keepdims=True)
        d_scores = (probs * (d_probs - delta)).astype(BF)
        q_pieces.append(dot_left(d_scores, k) * scale)
        k_pieces.append(dot_plain(d_scores, q) * scale)
        v_pieces.append(dot_plain(probs.astype(BF), g))
    out_ref[block, 0, :, :span] = jnp.concatenate(q_pieces, axis=-1).astype(BF)
    key_acc[...] += jnp.concatenate(k_pieces, axis=-1)
    value_acc[...] += jnp.concatenate(v_pieces, axis=-1)

    @pl.when(block == parts - 1)
    def _():
        out_ref[:, 0, :, span : 2 * span] = key_acc[...].astype(BF).reshape(parts, rows, span)
        out_ref[:, 0, :, 2 * span :] = value_acc[...].astype(BF).reshape(parts, rows, span)


def attention_backward(qkv, grads, lengths, per):
    parts, seqs, rows, _ = qkv.shape
    span = per * HEAD
    return pl.pallas_call(
        partial(attention_backward_kernel, per),
        grid_spec=pltpu.PrefetchScalarGridSpec(
            num_scalar_prefetch=1,
            grid=(seqs, parts),
            in_specs=[
                pl.BlockSpec((parts, 1, rows, 3 * span), lambda m, b, n: (0, m, 0, 0)),
                pl.BlockSpec((parts, 1, rows, span), lambda m, b, n: (0, m, 0, 0)),
            ],
            out_specs=pl.BlockSpec((parts, 1, rows, 3 * span), lambda m, b, n: (0, m, 0, 0)),
            scratch_shapes=[
                pltpu.VMEM((parts * rows, span), F32),
                pltpu.VMEM((parts * rows, span), F32),
            ],
        ),
        out_shape=jax.ShapeDtypeStruct(qkv.shape, BF),
        name="attend_backward",
    )(lengths, qkv, grads)


def exchange(blocks):
    return lax.all_to_all(blocks, "seq", split_axis=0, concat_axis=0)


def relocate(masks, value):
    levels = lax.axis_size("dp").bit_length() - 1
    for bit in range(levels):
        apart = 1 << bit
        pairs = [(source, source ^ apart) for source in range(lax.axis_size("dp"))]
        other = lax.ppermute(value, "dp", pairs)
        moving = (jnp.bitwise_and(masks, apart) != 0)[:, None, None]
        value = jnp.where(moving, other, value)
    return value


def edges(block):
    count = lax.axis_size("seq")
    forward = [(i, i + 1) for i in range(count - 1)]
    backward = [(target, source) for source, target in forward]
    low = lax.ppermute(block[:, -1:], "seq", forward)
    high = lax.ppermute(block[:, :1], "seq", backward)
    return low, high


def shifted(block, low, high):
    before = jnp.concatenate([low, block[:, :-1]], axis=1)
    after = jnp.concatenate([block[:, 1:], high], axis=1)
    flat = (-1, block.shape[-1])
    return before.reshape(flat), block.reshape(flat), after.reshape(flat)


def heads_first(weight, parts):
    rows = weight.shape[0]
    split = weight.reshape(rows, 3, parts, WIDE // parts)
    return split.transpose(0, 2, 1, 3).reshape(rows, 3 * WIDE)


def heads_last(weight, parts):
    rows = weight.shape[0]
    split = weight.reshape(rows, parts, 3, WIDE // parts)
    return split.transpose(0, 2, 1, 3).reshape(rows, 3 * WIDE)


def gather_weights(big, small):
    copies = [piece.astype(BF) for piece in big]
    sizes = [piece.size for piece in small]
    flat = jnp.concatenate([piece.reshape(-1) for piece in small]).astype(BF)
    columns = copies[0].shape[1]
    high = -(-flat.size // columns)
    high = -(-high // 8) * 8
    flat = jnp.pad(flat, (0, high * columns - flat.size)).reshape(high, columns)
    rows = copies[-1].shape[0]
    copies[-1] = jnp.concatenate([copies[-1], flat], axis=0)
    full = [lax.all_gather(piece, "dp", axis=0) for piece in copies]
    last = full[-1]
    full[-1] = last[:, :rows]
    full = [piece.reshape(-1, piece.shape[-1]) for piece in full]
    table = last[:, rows:].reshape(last.shape[0], -1)
    vectors = []
    start = 0
    for piece, size in zip(small, sizes):
        part = table[:, start : start + size]
        vectors.append(part.reshape((-1,) + piece.shape[1:]).astype(F32))
        start += size
    return full, vectors


def reduce_grads(big, small):
    groups = lax.axis_size("dp")
    blocks = []
    for grad in big:
        rows, columns = grad.shape
        for start in range(0, columns, WIDE):
            blocks.append(grad[:, start : start + WIDE].reshape(groups, rows // groups, WIDE))
    flat = jnp.concatenate([piece.reshape(groups, -1) for piece in small], axis=1)
    high = -(-flat.shape[1] // WIDE)
    high = -(-high // 16) * 16
    flat = jnp.pad(flat, ((0, 0), (0, high * WIDE - flat.shape[1])))
    blocks.append(flat.reshape(groups, high, WIDE))
    packed = jnp.concatenate([piece.astype(BF) for piece in blocks], axis=1)
    mine = lax.psum_scatter(packed, "dp", scatter_dimension=0, tiled=False)
    mine = lax.psum(mine, "seq").astype(F32)
    outs = []
    at = 0
    for grad in big:
        rows, columns = grad.shape[0] // groups, grad.shape[1]
        parts = []
        for _ in range(columns // WIDE):
            parts.append(mine[at : at + rows])
            at += rows
        outs.append(parts[0] if len(parts) == 1 else jnp.concatenate(parts, axis=1))
    tail = mine[at:].reshape(-1)
    start = 0
    for piece in small:
        size = piece.size // groups
        shape = (piece.shape[0] // groups,) + piece.shape[1:]
        outs.append(tail[start : start + size].reshape(shape))
        start += size
    return outs


def body(
    tokens,
    chars,
    char_counts,
    lengths,
    perm,
    token_cot,
    char_cot,
    w_qkv,
    b_qv,
    w_out,
    w_in,
    b_in,
    w_back,
    gru_x,
    gru_h,
    gru_bias,
    blend_w,
    conv_w,
    conv_b,
    norm_gain,
    norm_bias,
    row_bias,
):
    parts = lax.axis_size("seq")
    seqs, local, width = tokens.shape
    rows = seqs * local
    per = width // HEAD // parts
    three = 3 * H
    masks = perm[:, 0]
    place = lax.axis_index("dp")
    own_lengths = lax.dynamic_slice(lengths, (place * seqs,), (seqs,))
    cots = relocate(masks, jnp.concatenate([token_cot, char_cot], axis=-1))

    big = (heads_first(w_qkv, parts), gru_x, w_out, w_in, w_back, blend_w, conv_w, gru_h)
    small = (b_qv, b_in, gru_bias, conv_b, norm_gain, norm_bias, row_bias)
    full, vectors = gather_weights(big, small)
    w_qkv, gru_x, w_out, w_in, w_back, blend_w, conv_w, gru_h = full
    b_qv, b_in, gru_bias, conv_b, norm_gain, norm_bias, row_bias = vectors

    flat_tokens = tokens.reshape(rows, width)
    bias = jnp.concatenate([b_qv[:width], jnp.zeros((width,), F32), b_qv[width:]])
    bias = heads_first(bias[None], parts)[0]
    project = (dot_plain(flat_tokens, w_qkv) + bias).astype(BF)
    span = 3 * per * HEAD
    qkv = project.reshape(seqs, local, parts, span).transpose(2, 0, 1, 3)
    qkv = exchange(qkv)
    context = exchange(attention_forward(qkv, own_lengths, per))
    context = context.transpose(1, 2, 0, 3).reshape(rows, width)

    counts = char_counts.reshape(rows, 1)
    flat_chars = chars.transpose(2, 0, 1, 3).reshape(NCHAR * rows, width)
    gates = (dot_plain(flat_chars, gru_x) + gru_bias[:, 0]).reshape(NCHAR, rows, 2 * three)
    sides = []
    for side in range(2):
        columns = slice(side * three, (side + 1) * three)
        state = jnp.zeros((rows, H), F32)
        steps = []
        for order in range(NCHAR):
            position = order if side == 0 else NCHAR - 1 - order
            live = position < counts
            low = state.astype(BF)
            recur = dot_plain(low, gru_h[:, columns]) + gru_bias[columns, 1]
            steps.append((position, live, low, recur, state))
            state = gru_cell(live, gates[position, :, columns], recur, state)
        sides.append((state, steps))
    char_state = jnp.concatenate([sides[0][0], sides[1][0]], axis=-1)

    summed_first = flat_tokens.astype(F32) + dot_plain(context, w_out) + row_bias[:, 0]
    hidden1 = norm_rows(summed_first, norm_gain[:, 0], norm_bias[:, 0])
    hidden1_low = hidden1.astype(BF)
    inner = dot_plain(hidden1_low, w_in) + b_in
    activated = gelu_exact(inner).astype(BF)
    summed_second = hidden1 + dot_plain(activated, w_back) + row_bias[:, 1]
    hidden2 = norm_rows(summed_second, norm_gain[:, 1], norm_bias[:, 1])
    hidden2_low = hidden2.astype(BF)
    char_low = char_state.astype(BF)
    token_side = dot_plain(hidden2_low, blend_w[:, :width]) + row_bias[:, 2]
    char_side = dot_plain(char_low, blend_w[:, width:]) + row_bias[:, 3]
    joined = jnp.concatenate([token_side, char_side], axis=-1).astype(BF)
    joined = joined.reshape(seqs, local, 2 * width)
    taps = shifted(joined, *edges(joined))
    stacked = jnp.concatenate(taps, axis=-1)
    mixed = dot_plain(stacked, conv_w) + conv_b
    lifted = gelu_exact(mixed)
    token_pre = hidden2 + lifted[:, :width]
    char_pre = char_state + lifted[:, width:]
    token_out = norm_rows(token_pre, norm_gain[:, 2], norm_bias[:, 2]).astype(BF)
    char_out = norm_rows(char_pre, norm_gain[:, 3], norm_bias[:, 3]).astype(BF)
    outs = jnp.concatenate([token_out, char_out], axis=-1).reshape(seqs, local, 2 * width)
    outs = relocate(masks, outs)

    flat_cots = cots.reshape(rows, 2 * width).astype(F32)
    d_token_pre, gain_token, shift_token = norm_back(
        token_pre, norm_gain[:, 2], flat_cots[:, :width]
    )
    d_char_pre, gain_char, shift_char = norm_back(char_pre, norm_gain[:, 3], flat_cots[:, width:])
    d_mixed = jnp.concatenate([d_token_pre, d_char_pre], axis=-1) * gelu_slope(mixed)
    d_mixed = d_mixed.astype(BF)
    grad_conv = dot_left(stacked, d_mixed)
    beside = d_mixed.reshape(seqs, local, 2 * width)
    before, same, after = shifted(beside, *edges(beside))
    taps_w = conv_w.reshape(3, 2 * width, 2 * width)
    d_joined = dot_right(after, taps_w[0]) + dot_right(same, taps_w[1])
    d_joined = (d_joined + dot_right(before, taps_w[2])).astype(BF)
    d_token_side = d_joined[:, :width]
    d_char_side = d_joined[:, width:]
    grad_blend = jnp.concatenate(
        [dot_left(hidden2_low, d_token_side), dot_left(char_low, d_char_side)], axis=-1
    )
    d_hidden2 = d_token_pre + dot_right(d_token_side, blend_w[:, :width])
    d_char_state = d_char_pre + dot_right(d_char_side, blend_w[:, width:])

    d_second, gain_second, shift_second = norm_back(summed_second, norm_gain[:, 1], d_hidden2)
    d_branch = d_second.astype(BF)
    grad_back = dot_left(activated, d_branch)
    d_inner = (dot_right(d_branch, w_back) * gelu_slope(inner)).astype(BF)
    grad_in = dot_left(hidden1_low, d_inner)
    d_hidden1 = d_second + dot_right(d_inner, w_in)
    d_first, gain_first, shift_first = norm_back(summed_first, norm_gain[:, 0], d_hidden1)
    d_attend = d_first.astype(BF)
    grad_out = dot_left(context, d_attend)
    d_context = dot_right(d_attend, w_out).astype(BF)
    d_context = d_context.reshape(seqs, local, parts, per * HEAD).transpose(2, 0, 1, 3)
    d_project = exchange(attention_backward(qkv, exchange(d_context), own_lengths, per))
    d_project = d_project.transpose(1, 2, 0, 3).reshape(rows, 3 * width)

    d_gates = [[None, None] for _ in range(NCHAR)]
    grad_side, bias_side = [], []
    for side in range(2):
        columns = slice(side * three, (side + 1) * three)
        d_state = d_char_state[:, side * H : (side + 1) * H]
        lows, recurs = [], []
        for position, live, low, recur, state in reversed(sides[side][1]):
            _, pull = jax.vjp(
                partial(gru_cell, live), gates[position, :, columns], recur, state
            )
            d_gate, d_recur, d_keep = pull(d_state)
            d_recur = d_recur.astype(BF)
            lows.append(low)
            recurs.append(d_recur)
            d_state = d_keep + dot_right(d_recur, gru_h[:, columns])
            d_gates[position][side] = d_gate.astype(BF)
        lows, recurs = jnp.concatenate(lows, axis=0), jnp.concatenate(recurs, axis=0)
        grad_side.append(dot_left(lows, recurs))
        bias_side.append(column_sum(recurs))
    d_gates = jnp.concatenate([jnp.concatenate(pair, axis=-1) for pair in d_gates], axis=0)
    grad_gru_x = dot_left(flat_chars, d_gates)
    chars_back = dot_right(d_gates, gru_x).astype(BF)
    chars_back = chars_back.reshape(NCHAR, seqs, local, width).transpose(1, 2, 0, 3)
    grad_gru_h = jnp.concatenate(grad_side, axis=-1)
    grad_gru_bias = jnp.stack([column_sum(d_gates), jnp.concatenate(bias_side)], axis=-1)

    grad_qkv = dot_left(flat_tokens, d_project)
    sums = heads_last(column_sum(d_project)[None], parts)[0]
    grad_b_qv = jnp.concatenate([sums[:width], sums[2 * width :]])
    tokens_back = (d_first + dot_right(d_project, w_qkv)).astype(BF)
    grad_gain = jnp.stack([gain_first, gain_second, gain_token, gain_char], axis=-1)
    grad_shift = jnp.stack([shift_first, shift_second, shift_token, shift_char], axis=-1)
    grad_rows = jnp.stack(
        [
            column_sum(d_attend),
            column_sum(d_branch),
            column_sum(d_token_side),
            column_sum(d_char_side),
        ],
        axis=-1,
    )
    big = (grad_qkv, grad_gru_x, grad_out, grad_in, grad_back, grad_blend, grad_conv, grad_gru_h)
    small = (
        grad_b_qv,
        column_sum(d_inner),
        grad_gru_bias,
        column_sum(d_mixed),
        grad_gain,
        grad_shift,
        grad_rows,
    )
    summed = reduce_grads(big, small)
    g_qkv, g_gru_x, g_out, g_in, g_back, g_blend, g_conv, g_gru_h = summed[:8]
    g_b_qv, g_b_in, g_gru_bias, g_conv_b, g_gain, g_shift, g_rows = summed[8:]
    return (
        outs[..., :width],
        outs[..., width:],
        tokens_back.reshape(seqs, local, width),
        chars_back,
        heads_last(g_qkv, parts),
        g_b_qv,
        g_out,
        g_in,
        g_b_in,
        g_back,
        g_gru_x,
        g_gru_h,
        g_gru_bias,
        g_blend,
        g_conv,
        g_conv_b,
        g_gain,
        g_shift,
        g_rows,
    )


def solution(mesh):
    rows, vector, seq = P("dp", None), P("dp"), P("dp", "seq", None)
    weights = (
        rows,
        vector,
        rows,
        rows,
        vector,
        rows,
        rows,
        rows,
        rows,
        rows,
        rows,
        vector,
        rows,
        rows,
        rows,
    )
    return jax.shard_map(
        body,
        mesh=mesh,
        in_specs=(seq, P("dp", "seq", None, None), P("dp", "seq"), P(), P(), seq, seq) + weights,
        out_specs=(seq, seq, seq, P("dp", "seq", None, None)) + weights,
        check_vma=False,
    )
```

time: 2580 us -> 1240 us (0.48)
  blocking collectives: 1420 us -> 0 us
  waiting for transfers between devices: 218 us -> 504 us
  matrix products: 314 us -> 183 us
  other arithmetic: 211 us -> 113 us
  Pallas kernels: 0 us -> 56.9 us
    unnamed x2 -> x0, blocking collectives: 1160 us -> none
    all_gather x19 -> x0, blocking collectives: 261 us -> none  [the longest x1 32.4 us: body(): lax.all_gather(shards[6].astype(jnp.bfloat16), 'seq', axis=0, tiled=True)]
    reduce_scatter x2 -> x1, waiting for transfers between devices: 0.01 us -> 212 us  [reduce_grads(): mine = lax.psum_scatter(packed, 'dp', scatter_dimension=0, tiled=False)]
    psum x0 -> x1, waiting for transfers between devices: none -> 125 us  [reduce_grads(): mine = lax.psum(mine, 'seq').astype(F32)]
    ppermute x38 -> x10, waiting for transfers between devices: 213 us -> 97.2 us  [the longest x6 94.8 us: relocate(): other = lax.ppermute(value, 'dp', pairs)]
    dot_general x44 -> x16, matrix products: 167 us -> 81.6 us  [dot_plain(): return jnp.dot(left, right, preferred_element_type=F32)]
    reshape x25 -> x17, local copies, waits for them, and re-layouts: 107 us -> 30 us  [the longest x2 14.5 us: body(): qkv = project.reshape(seqs, local, parts, span).transpose(2, 0, 1, 3)]
    convert_element_type x2 -> x30, local copies, waits for them, and re-layouts: 2.83 us -> 68.9 us  [the longest x20 62.3 us: reduce_grads(): packed = jnp.concatenate([piece.astype(BF) for piece in blocks], axis=1)]
  transfers between devices with their start and end apart: 53 -> 24, of which waited for: 12 -> 11; matrix products, arithmetic and copies ran while one was open for 21% -> 26% of each run, Pallas kernels for 0% -> 2%
where the time goes in v1:
time: 1240 us; the launch traced here: 1230 us
  waiting for transfers between devices  504 us (41%)
  local copies, waits for them, and re-layouts  318 us (26%)
  matrix products  183 us (15%)
  other arithmetic  113 us (9%)
  Pallas kernels  56.9 us (5%)
  starting transfers between devices  34.3 us (3%)
  between operations  17.3 us (1%)
    reduce_scatter x1, waiting for transfers between devices, reduce_grads(): mine = lax.psum_scatter(packed, 'dp', scatter_dimension=0, tiled=False)  212 us
    psum x1, waiting for transfers between devices, reduce_grads(): mine = lax.psum(mine, 'seq').astype(F32)  125 us
    ppermute x6, waiting for transfers between devices, relocate(): other = lax.ppermute(value, 'dp', pairs)  94.8 us
    dot_general x16, matrix products, dot_plain(): return jnp.dot(left, right, preferred_element_type=F32)  81.6 us
    concatenate x1, local copies, waits for them, and re-layouts, reduce_grads(): packed = jnp.concatenate([piece.astype(BF) for piece in blocks], axis=1)  68.9 us
    convert_element_type x20, local copies, waits for them, and re-layouts, reduce_grads(): packed = jnp.concatenate([piece.astype(BF) for piece in blocks], axis=1)  62.3 us
    unnamed x378, local copies, waits for them, and re-layouts  53.5 us
    dot_general x16, matrix products, dot_right(): lax.dot_general(left, right, (((1,), (1,)), ((), ())), preferred_element_...  51.3 us
  transfers between devices with their start and end apart: 24, of which 11 were waited for; matrix products, arithmetic and copies ran while one was open for 26% of the time, Pallas kernels for 2%

profile of v1, /device:TPU:0, one launch (start us, length us, event | category | flops | bytes accessed | tf_op | source)
XLA Modules:
  0.0 1226.1 jit_solution(18305327372557792447)
XLA Ops:
  40.6 41.0 %collective-permute-done.6 = bf16[2,256,1536]{2,1,0:T(8,128)(2,1)S(1)} collective-permute-done((bf16[2,256,1536]{2,1,0:T(8,128)(2,1)S(1)}, bf16[2,256,1536]{2,1,0:T(8,128)(2,1)S(1)}, u32[]{:S(2)}, u32[]{:S(2)}) %collective-permute-start.6) | collective-permute-done | bytes 1572896 | tf_op jit(solution)/shard_map/ppermute | solution.py:184
  101.8 30.5 %collective-permute-done.7 = bf16[2,256,1536]{2,1,0:T(8,128)(2,1)} collective-permute-done((bf16[2,256,1536]{2,1,0:T(8,128)(2,1)}, bf16[2,256,1536]{2,1,0:T(8,128)(2,1)}, u32[]{:S(2)}, u32[]{:S(2)}) %collective-permute-start.7) | collective-permute-done | bytes 1572896 | tf_op jit(solution)/shard_map/ppermute | solution.py:184
  148.6 8.0 copy.264
  165.1 13.8 %convolution_add_fusion = f32[2048,2304]{1,0:T(8,128)} fusion(bf16[2048,768]{1,0:T(8,128)(2,1)} %bitcast.189, bf16[768,2304]{1,0:T(8,128)(2,1)} %all-gather.28.cloned.1.call-done, f32[2304]{0:T(1024)S(1)} %slice_reduce_fusion.2), kind=kOutput, calls=%fused_computation.1 | convolution fusion | flops 7252475904 | bytes 25568256 | tf_op jit(solution)/shard_map/dot_general | solution.py:19
  178.9 9.4 slice_bitcast_fusion.7
  209.9 8.0 all-to-all-done
  222.2 19.9 %attend_forward.1 = bf16[4,2,256,192]{3,2,1,0:T(8,128)(2,1)} custom-call(s32[2]{0:T(128)} %dynamic_slice.3.len_ref, bf16[4,2,256,576]{3,2,1,0:T(8,128)(2,1)} %copy.212.qkv_ref), custom_call_target="tpu_custom_call" | custom-call | tf_op jit(solution)/shard_map/attend_forward/pallas_call | solution.py:98
  260.4 7.9 all-to-all-done.1
  273.4 19.3 %fusion.2 = (bf16[512,3072]{1,0:T(8,128)(2,1)}, f32[512,3072]{1,0:T(8,128)}) fusion(f32[3072]{0:T(1024)S(1)} %reshape.483, bf16[768,3072]{1,0:T(8,128)(2,1)} %all-gather.22.cloned.1.call-done, f32[512,768]{1,0:T(8,128)S(1)} %get-tuple-element.297, f32[768]{0:T(1024)S(1)} %get-tuple-element.125, f32[768]{0:T(1024)S(1)} %get-tuple-element.121, ...), kind=kOutput, calls=%fused_computation.7 | convolution fusion | flops 2521694208 | bytes 15751168 | tf_op jit(solution)/shard_map/dot_general | solution.py:19
  309.1 50.3 %all-gather.30.cloned.1.call-done = bf16[4608,1536]{1,0:T(8,128)(2,1)} async-done(((bf16[576,1536]{1,0:T(8,128)(2,1)}), bf16[4608,1536]{1,0:T(8,128)(2,1)}) %all-gather.30.cloned.1.call-update) | async-done | bytes 14155792 | tf_op jit(solution)/shard_map/all_gather | solution.py:228
  359.4 19.8 %fusion.48 = (f32[512,1536]{1,0:T(8,128)S(1)}, f32[512,1536]{1,0:T(8,128)S(1)}) fusion(f32[1536]{0:T(1024)S(1)} %reshape.485, bf16[4608,1536]{1,0:T(8,128)(2,1)} %all-gather.30.cloned.1.call-done, bf16[512,1536]{1,0:T(8,128)(2,1)} %bitcast.205, bf16[512,768]{1,0:T(8,128)(2,1)S(1)} %copy-done.69, bf16[512,768]{1,0:T(8,128)(2,1)S(1)} %add_convert_fusion.4, ...), kind=kOutput, calls=%fused_computation.76 | convolution fusion | flops 7317749760 | bytes 25171968 | tf_op jit(solution)/shard_map/dot_general | solution.py:19
  387.4 13.1 %convolution_convert_fusion = bf16[4608,1536]{1,0:T(8,128)(2,1)} fusion(bf16[512,1536]{1,0:T(8,128)(2,1)S(1)} %get-tuple-element.138, bf16[512,1536]{1,0:T(8,128)(2,1)} %bitcast.206, bf16[512,768]{1,0:T(8,128)(2,1)} %add_convert_fusion.3, bf16[512,768]{1,0:T(8,128)(2,1)} %copy-done.70, bf16[512,1536]{1,0:T(8,128)(2,1)} %bitcast.204), kind=kOutput, calls=%fused_computation | convolution fusion | flops 7273709568 | bytes 20447232 | tf_op jit(solution)/shard_map/dot_general | solution.py:23
  406.4 10.0 fusion.324
  428.2 10.0 copy.241
  438.2 10.0 copy.242
  499.3 36.4 %maximum_maximum_fusion = bf16[2048,2304]{1,0:T(8,128)(2,1)} fusion(bf16[512,1152]{1,0:T(8,128)(2,1)S(1)} %fusion.85, bf16[512,1152]{1,0:T(8,128)(2,1)S(1)} %get-tuple-element.315, bf16[512,1152]{1,0:T(8,128)(2,1)S(1)} %fusion.83, bf16[512,1152]{1,0:T(8,128)(2,1)S(1)} %fusion.74, bf16[512,1152]{1,0:T(8,128)(2,1)S(1)} %fusion.81, ...), kind=kLoop, calls=%fused_computation.4 | loop fusion | flops 75497472 | bytes 18874368 | tf_op jit(solution)/shard_map/concatenate | solution.py:422
  537.8 7.4 fusion.341
  584.5 37.0 %attend_backward.1 = bf16[4,2,256,576]{3,2,1,0:T(8,128)(2,1)} custom-call(s32[2]{0:T(128)} %dynamic_slice.3.len_ref, bf16[4,2,256,576]{3,2,1,0:T(8,128)(2,1)} %copy.212.qkv_ref, bf16[4,2,256,192]{3,2,1,0:T(8,128)(2,1)} %copy.219.grad_ref), custom_call_target="tpu_custom_call" | custom-call | tf_op jit(solution)/shard_map/attend_backward/pallas_call | solution.py:155
  677.9 12.0 fusion.40
  718.8 68.9 %concatenate.147 = bf16[8,2944,768]{1,2,0:T(8,128)(2,1)} concatenate(bf16[8,96,768]{1,2,0:T(8,128)(2,1)} %copy.227, bf16[8,96,768]{1,2,0:T(8,128)(2,1)} %copy.228, bf16[8,96,768]{1,2,0:T(8,128)(2,1)} %copy.229, bf16[8,96,768]{1,2,0:T(8,128)(2,1)} %copy.230, bf16[8,96,768]{1,2,0:T(8,128)(2,1)} %copy.231, bf16[8,96,768]{1,2,0:T(8,128)(2,1)} %copy.232, bf16[8,96,768]{1,2,0:T(8,128)(2,1)} %copy.233, ...), dimensions={1} | concatenate | bytes 72351744 | tf_op jit(solution)/shard_map/concatenate | solution.py:254
  794.4 211.5 %reduce-scatter.2.cloned.1.call-done = bf16[1,2944,768]{1,2,0:T(8,128)(2,1)} async-done(((bf16[8,2944,768]{1,2,0:T(8,128)(2,1)}), bf16[1,2944,768]{1,2,0:T(8,128)(2,1)}) %reduce-scatter.2.cloned.1.call-update) | async-done | bytes 4522000 | tf_op jit(solution)/shard_map/reduce_scatter | solution.py:255
  1007.9 10.3 convolution_convert_fusion.5
  1022.4 19.9 %collective-permute-done.4 = bf16[2,256,1536]{2,1,0:T(8,128)(2,1)S(1)} collective-permute-done((bf16[2,256,1536]{2,1,0:T(8,128)(2,1)S(1)}, bf16[2,256,1536]{2,1,0:T(8,128)(2,1)S(1)}, u32[]{:S(2)}, u32[]{:S(2)}) %collective-permute-start.4) | collective-permute-done | bytes 1572896 | tf_op jit(solution)/shard_map/ppermute | solution.py:184
  1049.0 124.7 %all-reduce.36.cloned.1.call-done = bf16[2944,768]{0,1:T(8,128)(2,1)} async-done(((bf16[2944,768]{0,1:T(8,128)(2,1)}), bf16[2944,768]{0,1:T(8,128)(2,1)}) %all-reduce.36.cloned.1.call-update) | async-done | bytes 4522000 | tf_op jit(solution)/shard_map/psum | solution.py:256
  (701 shorter events, 409.7 us)
Async XLA Ops:
  7.2 77.2 %all-gather.18.cloned.1.call-start = ((), (), s32[]{:S(2)}) async-start(), calls=%async_computation.8 | async-start | bytes 2322432 | tf_op jit(solution)/shard_map/all_gather | solution.py:228
  15.1 121.5 %all-gather.16.cloned.1.call-start = ((), (), s32[]{:S(2)}) async-start(), calls=%async_computation.5 | async-start | bytes 3981312 | tf_op jit(solution)/shard_map/all_gather | solution.py:228
  17.7 147.4 %all-gather.28.cloned.1.call-start = ((), (), s32[]{:S(2)}) async-start(), calls=%async_computation.13 | async-start | bytes 3981312 | tf_op jit(solution)/shard_map/all_gather | solution.py:228
  18.6 238.6 %all-gather.26.cloned.1.call-start = ((), (), s32[]{:S(2)}) async-start(), calls=%async_computation.12 | async-start | bytes 2654208 | tf_op jit(solution)/shard_map/all_gather | solution.py:228
  20.6 250.0 %all-gather.20.cloned.1.call-start = ((), (), s32[]{:S(2)}) async-start(), calls=%async_computation.9 | async-start | bytes 1327104 | tf_op jit(solution)/shard_map/all_gather | solution.py:228
  21.3 252.1 %all-gather.22.cloned.1.call-start = ((), (), s32[]{:S(2)}) async-start(), calls=%async_computation.10 | async-start | bytes 5308416 | tf_op jit(solution)/shard_map/all_gather | solution.py:228
  22.3 270.4 %all-gather.24.cloned.1.call-start = ((), (), s32[]{:S(2)}) async-start(), calls=%async_computation.11 | async-start | bytes 5308416 | tf_op jit(solution)/shard_map/all_gather | solution.py:228
  23.3 336.1 %all-gather.30.cloned.1.call-start = ((), (), s32[]{:S(2)}) async-start(), calls=%async_computation.14 | async-start | bytes 15925248 | tf_op jit(solution)/shard_map/all_gather | solution.py:228
  26.0 4.2 collective-permute-start.5
  33.0 48.6 %collective-permute-start.6 = (bf16[2,256,1536]{2,1,0:T(8,128)(2,1)S(1)}, bf16[2,256,1536]{2,1,0:T(8,128)(2,1)S(1)}, u32[]{:S(2)}, u32[]{:S(2)}) collective-permute-start(bf16[2,256,1536]{2,1,0:T(8,128)(2,1)S(1)} %broadcast_select_fusion), channel_id=1, source_target_pairs={{0,8},{4,12},{8,0},{12,4},{16,24},{20,28},{24,16},{28,20},{1,9},{5... | collective-permute-start | bytes 4718600 | tf_op jit(solution)/shard_map/ppermute | solution.py:184
  83.0 49.4 %collective-permute-start.7 = (bf16[2,256,1536]{2,1,0:T(8,128)(2,1)}, bf16[2,256,1536]{2,1,0:T(8,128)(2,1)}, u32[]{:S(2)}, u32[]{:S(2)}) collective-permute-start(bf16[2,256,1536]{2,1,0:T(8,128)(2,1)} %broadcast_select_fusion.2), channel_id=1, source_target_pairs={{0,16},{4,20},{8,24},{12,28},{16,0},{20,4},{24,8},{28,12},{1,17},{... | collective-permute-start | bytes 4718600 | tf_op jit(solution)/shard_map/ppermute | solution.py:184
  160.0 57.9 %all-to-all-start = ((bf16[4,2,256,576]{2,3,1,0:T(8,128)(2,1)}), bf16[4,2,256,576]{2,3,1,0:T(8,128)(2,1)}, u32[]{:S(2)}, u32[]{:S(2)}) async-start(bf16[4,2,256,576]{2,3,1,0:T(8,128)(2,1)} %copy.211), calls=%async_computation | async-start | bytes 4718592 | tf_op jit(solution)/shard_map/all_to_all | solution.py:176
  244.4 24.0 %all-to-all-start.1 = ((bf16[4,2,256,192]{2,3,1,0:T(8,128)(2,1)}), bf16[4,2,256,192]{2,3,1,0:T(8,128)(2,1)}, u32[]{:S(2)}, u32[]{:S(2)}) async-start(bf16[4,2,256,192]{2,3,1,0:T(8,128)(2,1)} %copy.213), calls=%async_computation.1 | async-start | bytes 1572864 | tf_op jit(solution)/shard_map/all_to_all | solution.py:176
  300.4 3.5 collective-permute-start
  302.2 5.6 collective-permute-start.1
  400.6 54.1 %collective-permute-start.8 = (bf16[2,1,1536]{2,1,0:T(2,128)(2,1)S(1)}, bf16[2,1,1536]{2,1,0:T(2,128)(2,1)S(1)}, u32[]{:S(2)}, u32[]{:S(2)}) collective-permute-start(bf16[2,1,1536]{2,1,0:T(2,128)(2,1)S(1)} %get-tuple-element.263), channel_id=1, source_target_pairs={{1,0},{2,1},{3,2},{5,4},{6,5},{7,6},{9,8},{10,9},{11,10},{13,12},{... | collective-permute-start | bytes 18440 | tf_op jit(solution)/shard_map/ppermute | solution.py:195
  401.9 46.3 %collective-permute-start.9 = (bf16[2,1,1536]{2,1,0:T(2,128)(2,1)S(1)}, bf16[2,1,1536]{2,1,0:T(2,128)(2,1)S(1)}, u32[]{:S(2)}, u32[]{:S(2)}) collective-permute-start(bf16[2,1,1536]{2,1,0:T(2,128)(2,1)S(1)} %get-tuple-element.264), channel_id=1, source_target_pairs={{0,1},{1,2},{2,3},{4,5},{5,6},{6,7},{8,9},{9,10},{10,11},{12,13},{... | collective-permute-start | bytes 18440 | tf_op jit(solution)/shard_map/ppermute | solution.py:194
  559.1 24.1 %all-to-all-start.2 = ((bf16[4,2,256,192]{2,3,1,0:T(8,128)(2,1)}), bf16[4,2,256,192]{2,3,1,0:T(8,128)(2,1)S(1)}, u32[]{:S(2)}, u32[]{:S(2)}) async-start(bf16[4,2,256,192]{2,3,1,0:T(8,128)(2,1)} %copy.217), calls=%async_computation.2 | async-start | bytes 1572864 | tf_op jit(solution)/shard_map/all_to_all | solution.py:176
  625.9 76.5 %all-to-all-start.3 = ((bf16[4,2,256,576]{2,3,1,0:T(8,128)(2,1)}), bf16[4,2,256,576]{2,3,1,0:T(8,128)(2,1)S(1)}, u32[]{:S(2)}, u32[]{:S(2)}) async-start(bf16[4,2,256,576]{2,3,1,0:T(8,128)(2,1)} %copy.220), calls=%async_computation.3 | async-start | bytes 4718592 | tf_op jit(solution)/shard_map/all_to_all | solution.py:176
  629.7 376.3 %reduce-scatter.2.cloned.1.call-start = ((), (), s32[]{:S(2)}) async-start(), calls=%async_computation.6 | async-start | bytes 40697856 | tf_op jit(solution)/shard_map/reduce_scatter | solution.py:255
  787.7 386.0 %all-reduce.36.cloned.1.call-start = ((), (), s32[]{:S(2)}) async-start(), calls=%async_computation.7 | async-start | bytes 9043968 | tf_op jit(solution)/shard_map/psum | solution.py:256
  789.2 3.5 collective-permute-start.2
  792.9 213.1 %collective-permute-start.3 = (bf16[2,256,1536]{2,1,0:T(8,128)(2,1)S(1)}, bf16[2,256,1536]{2,1,0:T(8,128)(2,1)S(1)}, u32[]{:S(2)}, u32[]{:S(2)}) collective-permute-start(bf16[2,256,1536]{2,1,0:T(8,128)(2,1)S(1)} %broadcast_select_fusion.1), channel_id=1, source_target_pairs={{0,8},{4,12},{8,0},{12,4},{16,24},{20,28},{24,16},{28,20},{1,9},{5... | collective-permute-start | bytes 4718600 | tf_op jit(solution)/shard_map/ppermute | solution.py:184
  1006.2 36.0 %collective-permute-start.4 = (bf16[2,256,1536]{2,1,0:T(8,128)(2,1)S(1)}, bf16[2,256,1536]{2,1,0:T(8,128)(2,1)S(1)}, u32[]{:S(2)}, u32[]{:S(2)}) collective-permute-start(bf16[2,256,1536]{2,1,0:T(8,128)(2,1)S(1)} %broadcast_select_fusion.3), channel_id=1, source_target_pairs={{0,16},{4,20},{8,24},{12,28},{16,0},{20,4},{24,8},{28,12},{1,17},{... | collective-permute-start | bytes 4718600 | tf_op jit(solution)/shard_map/ppermute | solution.py:184
  (181 other events, 3010.7 us)
Sparse Core Ops, SparseCore 0:
  15.2 35.9 all-gather.17
  53.7 43.6 all-gather.15
  99.8 40.2 all-gather.27
  142.4 28.8 all-gather.25
  173.1 23.9 all-gather.19
  199.3 38.7 all-gather.21
  240.0 38.7 all-gather.23
  280.7 78.6 all-gather.29
  787.8 218.0 reduce-scatter.1
  1008.1 165.5 all-reduce.35

commit v2 on v1

--- a/solution.py
+++ b/solution.py
@@ -176,13 +176,15 @@
     return lax.all_to_all(blocks, "seq", split_axis=0, concat_axis=0)
 
 
-def relocate(masks, value):
+def relocate(masks, value, ties):
     levels = lax.axis_size("dp").bit_length() - 1
     for bit in range(levels):
         apart = 1 << bit
         pairs = [(source, source ^ apart) for source in range(lax.axis_size("dp"))]
         other = lax.ppermute(value, "dp", pairs)
         moving = (jnp.bitwise_and(masks, apart) != 0)[:, None, None]
+        tie = ties[min(bit, len(ties) - 1)]
+        other, value, _ = lax.optimization_barrier((other, value, tie))
         value = jnp.where(moving, other, value)
     return value
 
@@ -201,6 +203,270 @@
     after = jnp.concatenate([block[:, 1:], high], axis=1)
     flat = (-1, block.shape[-1])
     return before.reshape(flat), block.reshape(flat), after.reshape(flat)
+
+
+def sum_plan(shapes, high):
+    spans, start = [], 0
+    for rows, columns in shapes:
+        tall = rows // 8 // high
+        count = tall * (columns // WIDE)
+        spans.append((start, start + count, tall))
+        start += count
+    return spans, start
+
+
+def sum_kernel(spans, total, high, lag, slots, *refs):
+    count = len(spans)
+    ins, outs = refs[:count], refs[count : 2 * count]
+    own, rc, sc, s1a, s1b, r1a, r1b, r2a, r2b, s2, rz, sz, rm, tot = refs[2 * count : 2 * count + 14]
+    sems = refs[2 * count + 14]
+    credits = refs[2 * count + 15]
+    half = WIDE // 2
+    dp, z = lax.axis_index("dp"), lax.axis_index("seq")
+    core, x, y = dp % 2, (dp // 2) % 2, dp // 4
+    at_core = {"dp": dp + 1 - 2 * core}
+    at_x = {"dp": dp + 2 - 4 * x}
+    at_y = {"dp": dp + 4 - 8 * y}
+    outer = (z % 3) == 0
+    inner = (z % 3) != 0
+    at_inner = {"seq": 1 + z // 3}
+    at_middle = {"seq": (3 - z) % 4}
+    at_outer = {"seq": (z // 2) * 3}
+
+    barrier = pltpu.get_barrier_semaphore()
+
+    def greet(where):
+        pl.semaphore_signal(barrier, inc=1, device_id=where, device_id_type=pl.DeviceIdType.MESH)
+
+    greet(at_core)
+    greet(at_x)
+    greet(at_y)
+
+    @pl.when(outer)
+    def _():
+        greet(at_inner)
+        pl.semaphore_wait(barrier, 4)
+
+    @pl.when(inner)
+    def _():
+        greet(at_middle)
+        greet(at_outer)
+        pl.semaphore_wait(barrier, 5)
+
+    def remote(source, target, name, slot, where):
+        return pltpu.make_async_remote_copy(
+            src_ref=source,
+            dst_ref=target,
+            send_sem=sems.at[2 * name, slot],
+            recv_sem=sems.at[2 * name + 1, slot],
+            device_id=where,
+            device_id_type=pl.DeviceIdType.MESH,
+        )
+
+    CORE, X1, Y1, X2, Y2, OUTER, MIDDLE, FINAL, LOCAL = range(9)
+
+    def give_credit(name, k, where):
+        @pl.when(k + slots < total)
+        def _():
+            pl.semaphore_signal(
+                credits.at[name], inc=1, device_id=where, device_id_type=pl.DeviceIdType.MESH
+            )
+
+    def take_credit(name, k):
+        @pl.when(k >= slots)
+        def _():
+            pl.semaphore_wait(credits.at[name], 1)
+
+    def send_core(slot, source):
+        return remote(source, rc.at[slot], CORE, slot, at_core)
+
+    def send_x1(slot):
+        return remote(sc.at[slot, :, 1 - x, :, :half], r1a.at[slot], X1, slot, at_x)
+
+    def send_y1(slot):
+        return remote(sc.at[slot, 1 - y, :, :, half:], r1b.at[slot], Y1, slot, at_y)
+
+    def send_y2(slot):
+        return remote(s1a.at[slot, 1 - y], r2a.at[slot], Y2, slot, at_y)
+
+    def send_x2(slot):
+        return remote(s1b.at[slot, 1 - x], r2b.at[slot], X2, slot, at_x)
+
+    def send_outer(slot):
+        return remote(s2.at[slot], rz.at[slot], OUTER, slot, at_inner)
+
+    def send_middle(slot):
+        return remote(sz.at[slot], rm.at[slot], MIDDLE, slot, at_middle)
+
+    def send_final(slot, target):
+        return remote(tot.at[slot], target, FINAL, slot, at_outer)
+
+    def load(slot, source):
+        return pltpu.make_async_copy(source, own.at[slot], sems.at[2 * LOCAL, slot])
+
+    def save(slot, target):
+        return pltpu.make_async_copy(tot.at[slot], target, sems.at[2 * LOCAL + 1, slot])
+
+    def window(ref, j, tall):
+        return pl.ds((j % tall) * high, high), pl.ds((j // tall) * WIDE, WIDE)
+
+    def add(left, right):
+        return (left.astype(F32) + right.astype(F32)).astype(BF)
+
+    def stage(k, run):
+        @pl.when((k >= 0) & (k < total))
+        def _():
+            run(k, lax.rem(jnp.maximum(k, 0), slots))
+
+    first = ins[0].at[:, core, pl.ds(0, high), pl.ds(0, WIDE)]
+    final = outs[0].at[pl.ds(0, high), pl.ds(0, WIDE)]
+
+    @pl.loop(0, total + 6 * lag)
+    def _(t):
+        def begin(k, slot):
+            take_credit(CORE, k)
+            for (start, stop, tall), ref in zip(spans, ins):
+
+                @pl.when((k >= start) & (k < stop))
+                def _():
+                    rows, columns = window(ref, k - start, tall)
+                    send_core(slot, ref.at[:, 1 - core, rows, columns]).start()
+                    load(slot, ref.at[:, core, rows, columns]).start()
+
+        def add_core(k, slot):
+            load(slot, first).wait()
+            send_core(slot, first).wait()
+            both = add(own[slot], rc[slot])
+            sc[slot] = both.reshape(2, 2, high, WIDE)
+            give_credit(CORE, k, at_core)
+
+        def add_one(k, slot):
+            send_x1(slot).wait()
+            send_y1(slot).wait()
+            s1a[slot] = add(sc[slot, :, x, :, :half], r1a[slot])
+            s1b[slot] = add(sc[slot, y, :, :, half:], r1b[slot])
+            give_credit(X1, k, at_x)
+            give_credit(Y1, k, at_y)
+
+        def add_two(k, slot):
+            send_y2(slot).wait()
+            send_x2(slot).wait()
+            s2[slot, :, :half] = add(s1a[slot, y], r2a[slot])
+            s2[slot, :, half:] = add(s1b[slot, x], r2b[slot])
+            give_credit(Y2, k, at_y)
+            give_credit(X2, k, at_x)
+
+        def add_outer(k, slot):
+            @pl.when(outer)
+            def _():
+                send_outer(slot).wait_send()
+
+            @pl.when(inner)
+            def _():
+                send_outer(slot).wait_recv()
+                sz[slot] = add(s2[slot], rz[slot])
+                give_credit(OUTER, k, at_outer)
+
+        def add_middle(k, slot):
+            @pl.when(inner)
+            def _():
+                send_middle(slot).wait()
+                tot[slot] = add(sz[slot], rm[slot])
+                give_credit(MIDDLE, k, at_middle)
+
+        def finish(k, slot):
+            @pl.when(inner)
+            def _():
+                save(slot, final).wait()
+                send_final(slot, final).wait_send()
+
+            @pl.when(outer)
+            def _():
+                send_final(slot, final).wait_recv()
+                give_credit(FINAL, k, at_inner)
+
+        def go_one(k, slot):
+            take_credit(X1, k)
+            send_x1(slot).start()
+            take_credit(Y1, k)
+            send_y1(slot).start()
+
+        def go_two(k, slot):
+            take_credit(Y2, k)
+            send_y2(slot).start()
+            take_credit(X2, k)
+            send_x2(slot).start()
+
+        def go_outer(k, slot):
+            @pl.when(outer)
+            def _():
+                take_credit(OUTER, k)
+                send_outer(slot).start()
+
+        def go_middle(k, slot):
+            @pl.when(inner)
+            def _():
+                take_credit(MIDDLE, k)
+                send_middle(slot).start()
+
+        def go_final(k, slot):
+            @pl.when(inner)
+            def _():
+                take_credit(FINAL, k)
+                for (start, stop, tall), ref in zip(spans, outs):
+
+                    @pl.when((k >= start) & (k < stop))
+                    def _():
+                        rows, columns = window(ref, k - start, tall)
+                        save(slot, ref.at[rows, columns]).start()
+                        send_final(slot, ref.at[rows, columns]).start()
+
+        stage(t, begin)
+        stage(t - lag, add_core)
+        stage(t - 2 * lag, add_one)
+        stage(t - 3 * lag, add_two)
+        stage(t - 4 * lag, add_outer)
+        stage(t - 5 * lag, add_middle)
+        stage(t - lag, go_one)
+        stage(t - 2 * lag, go_two)
+        stage(t - 3 * lag, go_outer)
+        stage(t - 4 * lag, go_middle)
+        stage(t - 5 * lag, go_final)
+        stage(t - 6 * lag, finish)
+
+
+def sum_grads(grads, high=48, lag=2, slots=4):
+    shapes = [grad.shape for grad in grads]
+    spans, total = sum_plan(shapes, high)
+    half = WIDE // 2
+    anywhere = pl.BlockSpec(memory_space=pl.ANY)
+    blocks = [grad.reshape(4, 2, grad.shape[0] // 8, grad.shape[1]) for grad in grads]
+    return pl.pallas_call(
+        partial(sum_kernel, spans, total, high, lag, slots),
+        in_specs=[anywhere] * len(grads),
+        out_specs=[anywhere] * len(grads),
+        out_shape=[jax.ShapeDtypeStruct((rows // 8, columns), BF) for rows, columns in shapes],
+        scratch_shapes=[
+            pltpu.VMEM((slots, 4, high, WIDE), BF),
+            pltpu.VMEM((slots, 4, high, WIDE), BF),
+            pltpu.VMEM((slots, 2, 2, high, WIDE), BF),
+            pltpu.VMEM((slots, 2, high, half), BF),
+            pltpu.VMEM((slots, 2, high, half), BF),
+            pltpu.VMEM((slots, 2, high, half), BF),
+            pltpu.VMEM((slots, 2, high, half), BF),
+            pltpu.VMEM((slots, high, half), BF),
+            pltpu.VMEM((slots, high, half), BF),
+            pltpu.VMEM((slots, high, WIDE), BF),
+            pltpu.VMEM((slots, high, WIDE), BF),
+            pltpu.VMEM((slots, high, WIDE), BF),
+            pltpu.VMEM((slots, high, WIDE), BF),
+            pltpu.VMEM((slots, high, WIDE), BF),
+            pltpu.SemaphoreType.DMA((18, slots)),
+            pltpu.SemaphoreType.REGULAR((8,)),
+        ],
+        compiler_params=pltpu.CompilerParams(collective_id=1, has_side_effects=True),
+        name="sum_grads",
+    )(*blocks)
 
 
 def heads_first(weight, parts):
@@ -239,31 +505,42 @@
     return full, vectors
 
 
-def reduce_grads(big, small):
+def pack_small(small, groups, multiple):
+    flat = jnp.concatenate([piece.reshape(groups, -1) for piece in small], axis=1)
+    high = -(-flat.shape[1] // WIDE)
+    high = -(-high // multiple) * multiple
+    flat = jnp.pad(flat, ((0, 0), (0, high * WIDE - flat.shape[1])))
+    return flat.reshape(groups * high, WIDE).astype(BF)
+
+
+def sum_grads_plain(grads):
     groups = lax.axis_size("dp")
     blocks = []
-    for grad in big:
+    for grad in grads:
         rows, columns = grad.shape
         for start in range(0, columns, WIDE):
             blocks.append(grad[:, start : start + WIDE].reshape(groups, rows // groups, WIDE))
-    flat = jnp.concatenate([piece.reshape(groups, -1) for piece in small], axis=1)
-    high = -(-flat.shape[1] // WIDE)
-    high = -(-high // 16) * 16
-    flat = jnp.pad(flat, ((0, 0), (0, high * WIDE - flat.shape[1])))
-    blocks.append(flat.reshape(groups, high, WIDE))
-    packed = jnp.concatenate([piece.astype(BF) for piece in blocks], axis=1)
+    packed = jnp.concatenate(blocks, axis=1)
     mine = lax.psum_scatter(packed, "dp", scatter_dimension=0, tiled=False)
-    mine = lax.psum(mine, "seq").astype(F32)
-    outs = []
-    at = 0
-    for grad in big:
+    mine = lax.psum(mine, "seq")
+    outs, at = [], 0
+    for grad in grads:
         rows, columns = grad.shape[0] // groups, grad.shape[1]
         parts = []
         for _ in range(columns // WIDE):
             parts.append(mine[at : at + rows])
             at += rows
-        outs.append(parts[0] if len(parts) == 1 else jnp.concatenate(parts, axis=1))
-    tail = mine[at:].reshape(-1)
+        outs.append(jnp.concatenate(parts, axis=1))
+    return outs
+
+
+def reduce_grads(big, small):
+    groups = lax.axis_size("dp")
+    ours = groups == 8 and lax.axis_size("seq") == 4
+    grads = [grad.astype(BF) for grad in big] + [pack_small(small, groups, 48)]
+    outs = sum_grads(grads) if ours else sum_grads_plain(grads)
+    outs = [piece.astype(F32) for piece in outs]
+    tail = outs.pop().reshape(-1)
     start = 0
     for piece in small:
         size = piece.size // groups
@@ -305,8 +582,6 @@
     masks = perm[:, 0]
     place = lax.axis_index("dp")
     own_lengths = lax.dynamic_slice(lengths, (place * seqs,), (seqs,))
-    cots = relocate(masks, jnp.concatenate([token_cot, char_cot], axis=-1))
-
     big = (heads_first(w_qkv, parts), gru_x, w_out, w_in, w_back, blend_w, conv_w, gru_h)
     small = (b_qv, b_in, gru_bias, conv_b, norm_gain, norm_bias, row_bias)
     full, vectors = gather_weights(big, small)
@@ -341,6 +616,8 @@
         sides.append((state, steps))
     char_state = jnp.concatenate([sides[0][0], sides[1][0]], axis=-1)
 
+    cots = jnp.concatenate([token_cot, char_cot], axis=-1)
+    cots = relocate(masks, cots, (project, context, context))
     summed_first = flat_tokens.astype(F32) + dot_plain(context, w_out) + row_bias[:, 0]
     hidden1 = norm_rows(summed_first, norm_gain[:, 0], norm_bias[:, 0])
     hidden1_low = hidden1.astype(BF)
@@ -363,7 +640,6 @@
     token_out = norm_rows(token_pre, norm_gain[:, 2], norm_bias[:, 2]).astype(BF)
     char_out = norm_rows(char_pre, norm_gain[:, 3], norm_bias[:, 3]).astype(BF)
     outs = jnp.concatenate([token_out, char_out], axis=-1).reshape(seqs, local, 2 * width)
-    outs = relocate(masks, outs)
 
     flat_cots = cots.reshape(rows, 2 * width).astype(F32)
     d_token_pre, gain_token, shift_token = norm_back(
@@ -426,6 +702,7 @@
     grad_gru_h = jnp.concatenate(grad_side, axis=-1)
     grad_gru_bias = jnp.stack([column_sum(d_gates), jnp.concatenate(bias_side)], axis=-1)
 
+    outs = relocate(masks, outs, (d_joined, d_inner, d_context))
     grad_qkv = dot_left(flat_tokens, d_project)
     sums = heads_last(column_sum(d_project)[None], parts)[0]
     grad_b_qv = jnp.concatenate([sums[:width], sums[2 * width :]])

time: 1240 us -> 904 us (0.73)
  waiting for transfers between devices: 504 us -> 168 us
  local copies, waits for them, and re-layouts: 318 us -> 145 us
  Pallas kernels: 56.9 us -> 224 us
    reduce_scatter x1 -> x0, waiting for transfers between devices: 212 us -> none  [reduce_grads(): mine = lax.psum_scatter(packed, 'dp', scatter_dimension=0, tiled=False)]
    pallas_call x0 -> x1, Pallas kernels: none -> 167 us  [sum_grads(): pl.pallas_call(partial(sum_kernel, spans, total, high, lag, slots), in_sp...]
    psum x1 -> x0, waiting for transfers between devices: 125 us -> none  [reduce_grads(): mine = lax.psum(mine, 'seq').astype(F32)]
    all_gather x8, waiting for transfers between devices: 50.4 us -> 127 us  [gather_weights(): full = [lax.all_gather(piece, 'dp', axis=0) for piece in copies]]
    ppermute x6, waiting for transfers between devices: 94.8 us -> 22.2 us  [relocate(): other = lax.ppermute(value, 'dp', pairs)]
    concatenate x3 -> x2, local copies, waits for them, and re-layouts: 70.2 us -> 2.2 us  [the longest x1 2.11 us: body(): cots = jnp.concatenate([token_cot, char_cot], axis=-1)]
    convert_element_type x20 -> x0, local copies, waits for them, and re-layouts: 62.3 us -> none  [reduce_grads(): packed = jnp.concatenate([piece.astype(BF) for piece in blocks], axis=1)]
    slice x13 -> x0, local copies, waits for them, and re-layouts: 28 us -> none  [the longest x4 15.1 us: reduce_grads(): grad[:, start:start + WIDE].reshape(groups, rows // groups, WIDE)]
  transfers between devices with their start and end apart: 24 -> 22, of which waited for: 11 -> 11; matrix products, arithmetic and copies ran while one was open for 26% -> 37% of each run, Pallas kernels for 2% -> 6%
where the time goes in v2:
time: 904 us; the launch traced here: 899 us
  Pallas kernels  224 us (25%)
  matrix products  188 us (21%)
  waiting for transfers between devices  168 us (19%)
  local copies, waits for them, and re-layouts  145 us (16%)
  other arithmetic  121 us (13%)
  starting transfers between devices  36.1 us (4%)
  between operations  17 us (2%)
    pallas_call x1, Pallas kernels, sum_grads(): pl.pallas_call(partial(sum_kernel, spans, total, high, lag, slots), in_sp...  167 us
    all_gather x8, waiting for transfers between devices, gather_weights(): full = [lax.all_gather(piece, 'dp', axis=0) for piece in copies]  127 us
    dot_general x16, matrix products, dot_plain(): return jnp.dot(left, right, preferred_element_type=F32)  81.9 us
    dot_general x16, matrix products, dot_right(): lax.dot_general(left, right, (((1,), (1,)), ((), ())), preferred_element_...  55.2 us
    dot_general x10, matrix products, dot_left(): lax.dot_general(left, right, (((0,), (0,)), ((), ())), preferred_element_...  50.9 us
    unnamed x389, local copies, waits for them, and re-layouts  38 us
    pallas_call x1, Pallas kernels, attention_backward(): pl.pallas_call(partial(attention_backward_kernel, per), grid_spec=pltpu.P...  37.2 us
    concatenate x1, other arithmetic, body(): jnp.concatenate([jnp.concatenate(pair, axis=-1) for pair in d_gates], axi...  36.3 us
  transfers between devices with their start and end apart: 22, of which 11 were waited for; matrix products, arithmetic and copies ran while one was open for 37% of the time, Pallas kernels for 6%

profile of v2, /device:TPU:0, one launch (start us, length us, event | category | flops | bytes accessed | tf_op | source)
XLA Modules:
  0.0 899.2 jit_solution(3312481025840714066)
XLA Ops:
  34.4 11.2 %all-gather.18.cloned.1.call-done = bf16[448,2304]{1,0:T(8,128)(2,1)} async-done(((bf16[56,2304]{1,0:T(8,128)(2,1)}), bf16[448,2304]{1,0:T(8,128)(2,1)}) %all-gather.18.cloned.1.call-update) | async-done | bytes 2064400 | tf_op jit(solution)/shard_map/all_gather | solution.py:494
  63.5 18.5 %all-gather.16.cloned.1.call-done = bf16[8,96,2304]{2,1,0:T(8,128)(2,1)} async-done(((bf16[1,96,2304]{2,1,0:T(8,128)(2,1)}), bf16[8,96,2304]{2,1,0:T(8,128)(2,1)}) %all-gather.16.cloned.1.call-update) | async-done | bytes 3538960 | tf_op jit(solution)/shard_map/all_gather | solution.py:494
  87.4 6.6 reshape.516
  94.0 7.9 copy.150
  118.3 13.7 %convolution_add_fusion = f32[2048,2304]{1,0:T(8,128)} fusion(bf16[2048,768]{1,0:T(8,128)(2,1)} %bitcast.169, bf16[768,2304]{1,0:T(8,128)(2,1)} %all-gather.28.cloned.1.call-done, f32[2304]{0:T(1024)S(1)} %slice_reduce_fusion.2), kind=kOutput, calls=%fused_computation.1 | convolution fusion | flops 7252475904 | bytes 25568256 | tf_op jit(solution)/shard_map/dot_general | solution.py:19
  132.0 9.3 %slice_bitcast_fusion.7 = (f32[512,1152]{1,0:T(8,128)S(1)}, f32[512,1152]{1,0:T(8,128)S(1)}, f32[512,1152]{1,0:T(8,128)S(1)}, f32[512,1152]{1,0:T(8,128)}, f32[5...) fusion(f32[4,512,2304]{2,1,0:T(8,128)} %bitcast.147), kind=kLoop, calls=%fused_computation.154 | loop fusion | bytes 37748736 | tf_op jit(solution)/shard_map/squeeze | solution.py:615
  169.3 19.9 %attend_forward.1 = bf16[4,2,256,192]{3,2,1,0:T(8,128)(2,1)} custom-call(s32[2]{0:T(128)} %dynamic_slice.3.len_ref, bf16[4,2,256,576]{3,2,1,0:T(8,128)(2,1)} %copy.129.qkv_ref), custom_call_target="tpu_custom_call" | custom-call | tf_op jit(solution)/shard_map/attend_forward/pallas_call | solution.py:98
  207.4 8.1 all-to-all-done.1
  227.1 19.1 %fusion.2 = (bf16[512,3072]{1,0:T(8,128)(2,1)}, f32[512,3072]{1,0:T(8,128)}) fusion(f32[3072]{0:T(1024)S(1)} %reshape.486, bf16[768,3072]{1,0:T(8,128)(2,1)} %all-gather.22.cloned.1.call-done, f32[512,768]{1,0:T(8,128)S(1)} %get-tuple-element.306, f32[768]{0:T(1024)S(1)} %get-tuple-element.167, f32[768]{0:T(1024)S(1)} %get-tuple-element.163, ...), kind=kOutput, calls=%fused_computation.7 | convolution fusion | flops 2521694208 | bytes 15751168 | tf_op jit(solution)/shard_map/dot_general | solution.py:19
  246.2 32.3 %all-gather.24.cloned.1.call-done = bf16[3072,768]{1,0:T(8,128)(2,1)} async-done(((bf16[384,768]{1,0:T(8,128)(2,1)}), bf16[3072,768]{1,0:T(8,128)(2,1)}) %all-gather.24.cloned.1.call-update) | async-done | bytes 4718608 | tf_op jit(solution)/shard_map/all_gather | solution.py:494
  278.5 6.2 fusion.329
  299.3 59.7 %all-gather.30.cloned.1.call-done = bf16[4608,1536]{1,0:T(8,128)(2,1)} async-done(((bf16[576,1536]{1,0:T(8,128)(2,1)}), bf16[4608,1536]{1,0:T(8,128)(2,1)}) %all-gather.30.cloned.1.call-update) | async-done | bytes 14155792 | tf_op jit(solution)/shard_map/all_gather | solution.py:494
  359.1 20.1 %fusion.46 = (f32[512,1536]{1,0:T(8,128)S(1)}, f32[512,1536]{1,0:T(8,128)S(1)}) fusion(f32[1536]{0:T(1024)S(1)} %reshape.488, bf16[4608,1536]{1,0:T(8,128)(2,1)} %all-gather.30.cloned.1.call-done, bf16[512,1536]{1,0:T(8,128)(2,1)} %bitcast.184, bf16[512,768]{1,0:T(8,128)(2,1)} %add_convert_fusion.3, bf16[512,768]{1,0:T(8,128)(2,1)} %copy-done.74, ...), kind=kOutput, calls=%fused_computation.73 | convolution fusion | flops 7317749760 | bytes 25171968 | tf_op jit(solution)/shard_map/dot_general | solution.py:19
  388.1 11.6 %convolution_convert_fusion = bf16[4608,1536]{1,0:T(8,128)(2,1)} fusion(bf16[512,1536]{1,0:T(8,128)(2,1)S(1)} %get-tuple-element.180, bf16[512,1536]{1,0:T(8,128)(2,1)S(1)} %bitcast.185, bf16[512,768]{1,0:T(8,128)(2,1)S(1)} %copy-done.73, bf16[512,768]{1,0:T(8,128)(2,1)S(1)} %copy-done.75, bf16[512,1536]{1,0:T(8,128)(2,1)S(1)} %bitcast.183), kind=kOutput, calls=%fused_computation | convolution fusion | flops 7273709568 | bytes 20447232 | tf_op jit(solution)/shard_map/dot_general | solution.py:23
  467.4 36.3 %maximum_maximum_fusion = bf16[2048,2304]{1,0:T(8,128)(2,1)} fusion(bf16[512,1152]{1,0:T(8,128)(2,1)S(1)} %fusion.83, bf16[512,1152]{1,0:T(8,128)(2,1)S(1)} %get-tuple-element.324, bf16[512,1152]{1,0:T(8,128)(2,1)S(1)} %fusion.81, bf16[512,1152]{1,0:T(8,128)(2,1)S(1)} %fusion.72, bf16[512,1152]{1,0:T(8,128)(2,1)S(1)} %fusion.79, ...), kind=kLoop, calls=%fused_computation.4 | loop fusion | flops 75497472 | bytes 18874368 | tf_op jit(solution)/shard_map/concatenate | solution.py:698
  506.6 8.0 fusion.330
  550.7 8.9 convolution_convert_fusion.5
  576.0 37.2 %attend_backward.1 = bf16[4,2,256,576]{3,2,1,0:T(8,128)(2,1)} custom-call(s32[2]{0:T(128)} %dynamic_slice.3.len_ref, bf16[4,2,256,576]{3,2,1,0:T(8,128)(2,1)} %copy.129.qkv_ref, bf16[4,2,256,192]{3,2,1,0:T(8,128)(2,1)} %copy.136.grad_ref), custom_call_target="tpu_custom_call" | custom-call | tf_op jit(solution)/shard_map/attend_backward/pallas_call | solution.py:155
  625.4 6.0 copy.160
  634.2 13.2 %convolution_convert_fusion.1 = bf16[2304,768]{0,1:T(8,128)(2,1)} fusion(bf16[2048,2304]{1,0:T(8,128)(2,1)} %maximum_maximum_fusion, bf16[2048,768]{1,0:T(8,128)(2,1)S(1)} %bitcast.170), kind=kOutput, calls=%fused_computation.29 | convolution fusion | flops 7249526784 | bytes 16121856 | tf_op jit(solution)/shard_map/dot_general | solution.py:23
  647.4 22.2 %collective-permute-done.9 = bf16[2,256,1536]{2,1,0:T(8,128)(2,1)S(1)} collective-permute-done((bf16[2,256,1536]{2,1,0:T(8,128)(2,1)S(1)}, bf16[2,256,1536]{2,1,0:T(8,128)(2,1)S(1)}, u32[]{:S(2)}, u32[]{:S(2)}) %collective-permute-start.9) | collective-permute-done | bytes 1572896 | tf_op jit(solution)/shard_map/ppermute | solution.py:184
  685.8 167.0 %sum_grads.1 = (bf16[96,2304]{1,0:T(8,128)(2,1)}, bf16[96,2304]{1,0:T(8,128)(2,1)}, bf16[96,768]{1,0:T(8,128)(2,1)}, bf16[96,3072]{1,0:T(8,128)(2,1)}, bf16[384,...) custom-call(bf16[4,2,96,2304]{3,2,1,0:T(8,128)(2,1)} %bitcast.162, ...), custom_call_target="tpu_custom_call" | custom-call | tf_op jit(solution)/shard_map/sum_grads/pallas_call | solution.py:444
  852.8 12.0 %slice.563 = f32[18432,2]{1,0:T(8,128)} reshape(bf16[48,768]{1,0:T(8,128)(2,1)} %get-tuple-element.53) | data formatting | bytes 221184 | tf_op jit(solution)/shard_map/slice | solution.py:548
  864.8 6.2 slice.566
  (677 shorter events, 321.2 us)
Async XLA Ops:
  7.2 38.4 %all-gather.18.cloned.1.call-start = ((), (), s32[]{:S(2)}) async-start(), calls=%async_computation.5 | async-start | bytes 2322432 | tf_op jit(solution)/shard_map/all_gather | solution.py:494
  15.1 66.8 %all-gather.16.cloned.1.call-start = ((), (), s32[]{:S(2)}) async-start(), calls=%async_computation.4 | async-start | bytes 3981312 | tf_op jit(solution)/shard_map/all_gather | solution.py:494
  17.7 100.6 %all-gather.28.cloned.1.call-start = ((), (), s32[]{:S(2)}) async-start(), calls=%async_computation.10 | async-start | bytes 3981312 | tf_op jit(solution)/shard_map/all_gather | solution.py:494
  18.6 185.6 %all-gather.26.cloned.1.call-start = ((), (), s32[]{:S(2)}) async-start(), calls=%async_computation.9 | async-start | bytes 2654208 | tf_op jit(solution)/shard_map/all_gather | solution.py:494
  19.4 202.6 %all-gather.20.cloned.1.call-start = ((), (), s32[]{:S(2)}) async-start(), calls=%async_computation.6 | async-start | bytes 1327104 | tf_op jit(solution)/shard_map/all_gather | solution.py:494
  20.2 206.9 %all-gather.22.cloned.1.call-start = ((), (), s32[]{:S(2)}) async-start(), calls=%async_computation.7 | async-start | bytes 5308416 | tf_op jit(solution)/shard_map/all_gather | solution.py:494
  22.6 255.9 %all-gather.24.cloned.1.call-start = ((), (), s32[]{:S(2)}) async-start(), calls=%async_computation.8 | async-start | bytes 5308416 | tf_op jit(solution)/shard_map/all_gather | solution.py:494
  24.8 334.3 %all-gather.30.cloned.1.call-start = ((), (), s32[]{:S(2)}) async-start(), calls=%async_computation.11 | async-start | bytes 15925248 | tf_op jit(solution)/shard_map/all_gather | solution.py:494
  31.0 79.5 %collective-permute-start.3 = (bf16[2,256,1536]{2,1,0:T(8,128)(2,1)}, bf16[2,256,1536]{2,1,0:T(8,128)(2,1)}, u32[]{:S(2)}, u32[]{:S(2)}) collective-permute-start(bf16[2,256,1536]{2,1,0:T(8,128)(2,1)} %constant_dynamic-update-slice_fusion), channel_id=1, source_target_pairs={{0,4},{4,0},{8,12},{12,8},{16,20},{20,16},{24,28},{28,24},{1,5},{5... | collective-permute-start | bytes 4718600 | tf_op jit(solution)/shard_map/ppermute | solution.py:184
  34.4 262.8 %copy-start.157 = (pred[2]{0:T(512)(128)(4,1)}, pred[2]{0:T(512)(128)(4,1)S(1)}, u32[]{:S(2)}) copy-start(pred[2]{0:T(512)(128)(4,1)S(1)} %get-tuple-element.172) | copy-start | bytes 10
  56.8 221.7 %copy-start.133 = (f32[768]{0:T(1024)}, f32[768]{0:T(1024)S(1)}, u32[]{:S(2)}) copy-start(f32[768]{0:T(1024)S(1)} %get-tuple-element.163) | copy-start | bytes 9220
  105.3 59.7 %all-to-all-start = ((bf16[4,2,256,576]{2,3,1,0:T(8,128)(2,1)}), bf16[4,2,256,576]{2,3,1,0:T(8,128)(2,1)}, u32[]{:S(2)}, u32[]{:S(2)}) async-start(bf16[4,2,256,576]{2,3,1,0:T(8,128)(2,1)} %copy.128), calls=%async_computation | async-start | bytes 4718592 | tf_op jit(solution)/shard_map/all_to_all | solution.py:176
  113.8 104.7 %collective-permute-start.4 = (bf16[2,256,1536]{2,1,0:T(8,128)(2,1)}, bf16[2,256,1536]{2,1,0:T(8,128)(2,1)}, u32[]{:S(2)}, u32[]{:S(2)}) collective-permute-start(bf16[2,256,1536]{2,1,0:T(8,128)(2,1)} %broadcast_select_fusion.1), channel_id=1, source_target_pairs={{0,8},{4,12},{8,0},{12,4},{16,24},{20,28},{24,16},{28,20},{1,9},{5... | collective-permute-start | bytes 4718600 | tf_op jit(solution)/shard_map/ppermute | solution.py:184
  191.4 24.1 %all-to-all-start.1 = ((bf16[4,2,256,192]{2,3,1,0:T(8,128)(2,1)}), bf16[4,2,256,192]{2,3,1,0:T(8,128)(2,1)}, u32[]{:S(2)}, u32[]{:S(2)}) async-start(bf16[4,2,256,192]{2,3,1,0:T(8,128)(2,1)} %copy.130), calls=%async_computation.1 | async-start | bytes 1572864 | tf_op jit(solution)/shard_map/all_to_all | solution.py:176
  220.7 76.5 %collective-permute-start.5 = (bf16[2,256,1536]{2,1,0:T(8,128)(2,1)S(1)}, bf16[2,256,1536]{2,1,0:T(8,128)(2,1)}, u32[]{:S(2)}, u32[]{:S(2)}) collective-permute-start(bf16[2,256,1536]{2,1,0:T(8,128)(2,1)S(1)} %broadcast_select_fusion.3), channel_id=1, source_target_pairs={{0,16},{4,20},{8,24},{12,28},{16,0},{20,4},{24,8},{28,12},{1,17},{... | collective-permute-start | bytes 4718600 | tf_op jit(solution)/shard_map/ppermute | solution.py:184
  286.4 5.2 collective-permute-start
  290.3 5.6 collective-permute-start.1
  399.7 20.8 %collective-permute-start.6 = (bf16[2,1,1536]{2,1,0:T(2,128)(2,1)S(1)}, bf16[2,1,1536]{2,1,0:T(2,128)(2,1)S(1)}, u32[]{:S(2)}, u32[]{:S(2)}) collective-permute-start(bf16[2,1,1536]{2,1,0:T(2,128)(2,1)S(1)} %get-tuple-element.277), channel_id=1, source_target_pairs={{1,0},{2,1},{3,2},{5,4},{6,5},{7,6},{9,8},{10,9},{11,10},{13,12},{... | collective-permute-start | bytes 18440 | tf_op jit(solution)/shard_map/ppermute | solution.py:197
  401.0 14.5 %collective-permute-start.7 = (bf16[2,1,1536]{2,1,0:T(2,128)(2,1)S(1)}, bf16[2,1,1536]{2,1,0:T(2,128)(2,1)S(1)}, u32[]{:S(2)}, u32[]{:S(2)}) collective-permute-start(bf16[2,1,1536]{2,1,0:T(2,128)(2,1)S(1)} %get-tuple-element.278), channel_id=1, source_target_pairs={{0,1},{1,2},{2,3},{4,5},{5,6},{6,7},{8,9},{9,10},{10,11},{12,13},{... | collective-permute-start | bytes 18440 | tf_op jit(solution)/shard_map/ppermute | solution.py:196
  410.5 149.2 %collective-permute-start.2 = (bf16[2,256,1536]{2,1,0:T(8,128)(2,1)S(1)}, bf16[2,256,1536]{2,1,0:T(8,128)(2,1)}, u32[]{:S(2)}, u32[]{:S(2)}) collective-permute-start(bf16[2,256,1536]{2,1,0:T(8,128)(2,1)S(1)} %bitcast.155), channel_id=1, source_target_pairs={{0,4},{4,0},{8,12},{12,8},{16,20},{20,16},{24,28},{28,24},{1,5},{5... | collective-permute-start | bytes 4718600 | tf_op jit(solution)/shard_map/ppermute | solution.py:184
  533.7 40.1 %all-to-all-start.2 = ((bf16[4,2,256,192]{2,3,1,0:T(8,128)(2,1)}), bf16[4,2,256,192]{2,3,1,0:T(8,128)(2,1)}, u32[]{:S(2)}, u32[]{:S(2)}) async-start(bf16[4,2,256,192]{2,3,1,0:T(8,128)(2,1)} %copy.134), calls=%async_computation.2 | async-start | bytes 1572864 | tf_op jit(solution)/shard_map/all_to_all | solution.py:176
  562.6 68.8 %collective-permute-start.8 = (bf16[2,256,1536]{2,1,0:T(8,128)(2,1)}, bf16[2,256,1536]{2,1,0:T(8,128)(2,1)}, u32[]{:S(2)}, u32[]{:S(2)}) collective-permute-start(bf16[2,256,1536]{2,1,0:T(8,128)(2,1)} %broadcast_select_fusion), channel_id=1, source_target_pairs={{0,8},{4,12},{8,0},{12,4},{16,24},{20,28},{24,16},{28,20},{1,9},{5... | collective-permute-start | bytes 4718600 | tf_op jit(solution)/shard_map/ppermute | solution.py:184
  617.6 59.1 %all-to-all-start.3 = ((bf16[4,2,256,576]{2,3,1,0:T(8,128)(2,1)}), bf16[4,2,256,576]{2,3,1,0:T(8,128)(2,1)S(1)}, u32[]{:S(2)}, u32[]{:S(2)}) async-start(bf16[4,2,256,576]{2,3,1,0:T(8,128)(2,1)} %copy.137), calls=%async_computation.3 | async-start | bytes 4718592 | tf_op jit(solution)/shard_map/all_to_all | solution.py:176
  633.6 36.0 %collective-permute-start.9 = (bf16[2,256,1536]{2,1,0:T(8,128)(2,1)S(1)}, bf16[2,256,1536]{2,1,0:T(8,128)(2,1)S(1)}, u32[]{:S(2)}, u32[]{:S(2)}) collective-permute-start(bf16[2,256,1536]{2,1,0:T(8,128)(2,1)S(1)} %broadcast_select_fusion.2), channel_id=1, source_target_pairs={{0,16},{4,20},{8,24},{12,28},{16,0},{20,4},{24,8},{28,12},{1,17},{... | collective-permute-start | bytes 4718600 | tf_op jit(solution)/shard_map/ppermute | solution.py:184
  (187 other events, 2681.2 us)
Sparse Core Ops, SparseCore 0:
  15.2 30.3 all-gather.17
  48.1 33.8 all-gather.15
  84.4 33.8 all-gather.27
  120.6 38.3 all-gather.25
  160.7 23.9 all-gather.19
  187.0 40.0 all-gather.21
  229.0 49.4 all-gather.23
  280.4 78.6 all-gather.29

commit v3 on v2

--- a/solution.py
+++ b/solution.py
@@ -176,13 +176,19 @@
     return lax.all_to_all(blocks, "seq", split_axis=0, concat_axis=0)
 
 
+def relocate_step(masks, value, bit):
+    count = lax.axis_size("dp")
+    apart = 1 << bit
+    pairs = [(source, source ^ apart) for source in range(count)]
+    other = lax.ppermute(value, "dp", pairs)
+    moving = (jnp.bitwise_and(masks, apart) != 0)[:, None, None]
+    return other, value, moving
+
+
 def relocate(masks, value, ties):
     levels = lax.axis_size("dp").bit_length() - 1
     for bit in range(levels):
-        apart = 1 << bit
-        pairs = [(source, source ^ apart) for source in range(lax.axis_size("dp"))]
-        other = lax.ppermute(value, "dp", pairs)
-        moving = (jnp.bitwise_and(masks, apart) != 0)[:, None, None]
+        other, value, moving = relocate_step(masks, value, bit)
         tie = ties[min(bit, len(ties) - 1)]
         other, value, _ = lax.optimization_barrier((other, value, tie))
         value = jnp.where(moving, other, value)
@@ -198,6 +204,18 @@
     return low, high
 
 
+LINE = ([(0, 1), (3, 2)], [(1, 2), (2, 1)], [(1, 0), (2, 3)])
+
+
+def line_sum(value, step):
+    if lax.axis_size("seq") != 4:
+        return lax.psum(value, "seq") if step == 0 else value
+    other = lax.ppermute(value, "seq", LINE[step])
+    if step < 2:
+        return value + other
+    return jnp.where((lax.axis_index("seq") % 3) == 0, other, value)
+
+
 def shifted(block, low, high):
     before = jnp.concatenate([low, block[:, :-1]], axis=1)
     after = jnp.concatenate([block[:, 1:], high], axis=1)
@@ -208,19 +226,23 @@
 def sum_plan(shapes, high):
     spans, start = [], 0
     for rows, columns in shapes:
-        tall = rows // 8 // high
+        tall = rows // high
         count = tall * (columns // WIDE)
         spans.append((start, start + count, tall))
         start += count
     return spans, start
 
 
-def sum_kernel(spans, total, high, lag, slots, *refs):
-    count = len(spans)
+def sum_kernel(spans, pre_spans, late, pre, high, lag, slots, *refs):
+    whole = len(spans)
+    count = whole + len(pre_spans)
+    total = late + pre
     ins, outs = refs[:count], refs[count : 2 * count]
-    own, rc, sc, s1a, s1b, r1a, r1b, r2a, r2b, s2, rz, sz, rm, tot = refs[2 * count : 2 * count + 14]
-    sems = refs[2 * count + 14]
-    credits = refs[2 * count + 15]
+    own, rc, sc, s1a, s1b, r1a, r1b, r2a, r2b, s2, rz, sz, rm, tot, ready = refs[
+        2 * count : 2 * count + 15
+    ]
+    sems = refs[2 * count + 15]
+    credits = refs[2 * count + 16]
     half = WIDE // 2
     dp, z = lax.axis_index("dp"), lax.axis_index("seq")
     core, x, y = dp % 2, (dp // 2) % 2, dp // 4
@@ -263,7 +285,7 @@
             device_id_type=pl.DeviceIdType.MESH,
         )
 
-    CORE, X1, Y1, X2, Y2, OUTER, MIDDLE, FINAL, LOCAL = range(9)
+    CORE, X1, Y1, X2, Y2, OUTER, MIDDLE, FINAL, LOCAL, READY = range(10)
 
     def give_credit(name, k, where):
         @pl.when(k + slots < total)
@@ -304,11 +326,33 @@
     def load(slot, source):
         return pltpu.make_async_copy(source, own.at[slot], sems.at[2 * LOCAL, slot])
 
+    def load_ready(slot, source):
+        return pltpu.make_async_copy(source, ready.at[slot], sems.at[2 * READY, slot])
+
     def save(slot, target):
         return pltpu.make_async_copy(tot.at[slot], target, sems.at[2 * LOCAL + 1, slot])
 
     def window(ref, j, tall):
         return pl.ds((j % tall) * high, high), pl.ds((j // tall) * WIDE, WIDE)
+
+    def is_pre(k):
+        return (k < 3 * pre) & (k % 3 == 2)
+
+    def late_index(k):
+        return jnp.where(k < 3 * pre, (k // 3) * 2 + k % 3, k - pre)
+
+    def each(k, plan, parts, index, run):
+        for (start, stop, tall), ref in zip(plan, parts):
+
+            @pl.when((index >= start) & (index < stop))
+            def _():
+                run(ref, *window(ref, index - start, tall))
+
+    def on_late(k, run):
+        pl.when(jnp.logical_not(is_pre(k)))(run)
+
+    def on_pre(k, run):
+        pl.when(is_pre(k))(run)
 
     def add(left, right):
         return (left.astype(F32) + right.astype(F32)).astype(BF)
@@ -320,39 +364,56 @@
 
     first = ins[0].at[:, core, pl.ds(0, high), pl.ds(0, WIDE)]
     final = outs[0].at[pl.ds(0, high), pl.ds(0, WIDE)]
+    early = ins[whole].at[pl.ds(0, high), pl.ds(0, WIDE)]
 
     @pl.loop(0, total + 6 * lag)
     def _(t):
         def begin(k, slot):
             take_credit(CORE, k)
-            for (start, stop, tall), ref in zip(spans, ins):
-
-                @pl.when((k >= start) & (k < stop))
-                def _():
-                    rows, columns = window(ref, k - start, tall)
+
+            def go():
+                def run(ref, rows, columns):
                     send_core(slot, ref.at[:, 1 - core, rows, columns]).start()
                     load(slot, ref.at[:, core, rows, columns]).start()
 
+                each(k, spans, ins[:whole], late_index(k), run)
+
+            on_late(k, go)
+
         def add_core(k, slot):
-            load(slot, first).wait()
-            send_core(slot, first).wait()
-            both = add(own[slot], rc[slot])
-            sc[slot] = both.reshape(2, 2, high, WIDE)
+            def go():
+                load(slot, first).wait()
+                send_core(slot, first).wait()
+                both = add(own[slot], rc[slot])
+                sc[slot] = both.reshape(2, 2, high, WIDE)
+
+            on_late(k, go)
             give_credit(CORE, k, at_core)
 
         def add_one(k, slot):
-            send_x1(slot).wait()
-            send_y1(slot).wait()
-            s1a[slot] = add(sc[slot, :, x, :, :half], r1a[slot])
-            s1b[slot] = add(sc[slot, y, :, :, half:], r1b[slot])
+            def go():
+                send_x1(slot).wait()
+                send_y1(slot).wait()
+                s1a[slot] = add(sc[slot, :, x, :, :half], r1a[slot])
+                s1b[slot] = add(sc[slot, y, :, :, half:], r1b[slot])
+
+            on_late(k, go)
             give_credit(X1, k, at_x)
             give_credit(Y1, k, at_y)
 
         def add_two(k, slot):
-            send_y2(slot).wait()
-            send_x2(slot).wait()
-            s2[slot, :, :half] = add(s1a[slot, y], r2a[slot])
-            s2[slot, :, half:] = add(s1b[slot, x], r2b[slot])
+            def go():
+                send_y2(slot).wait()
+                send_x2(slot).wait()
+                s2[slot, :, :half] = add(s1a[slot, y], r2a[slot])
+                s2[slot, :, half:] = add(s1b[slot, x], r2b[slot])
+
+            def take():
+                load_ready(slot, early).wait()
+                s2[slot] = ready[slot]
+
+            on_late(k, go)
+            on_pre(k, take)
             give_credit(Y2, k, at_y)
             give_credit(X2, k, at_x)
 
@@ -387,15 +448,30 @@
 
         def go_one(k, slot):
             take_credit(X1, k)
-            send_x1(slot).start()
             take_credit(Y1, k)
-            send_y1(slot).start()
+
+            def go():
+                send_x1(slot).start()
+                send_y1(slot).start()
+
+            on_late(k, go)
 
         def go_two(k, slot):
             take_credit(Y2, k)
-            send_y2(slot).start()
             take_credit(X2, k)
-            send_x2(slot).start()
+
+            def go():
+                send_y2(slot).start()
+                send_x2(slot).start()
+
+            def fetch():
+                def run(ref, rows, columns):
+                    load_ready(slot, ref.at[rows, columns]).start()
+
+                each(k, pre_spans, ins[whole:], k // 3, run)
+
+            on_late(k, go)
+            on_pre(k, fetch)
 
         def go_outer(k, slot):
             @pl.when(outer)
@@ -413,13 +489,13 @@
             @pl.when(inner)
             def _():
                 take_credit(FINAL, k)
-                for (start, stop, tall), ref in zip(spans, outs):
-
-                    @pl.when((k >= start) & (k < stop))
-                    def _():
-                        rows, columns = window(ref, k - start, tall)
-                        save(slot, ref.at[rows, columns]).start()
-                        send_final(slot, ref.at[rows, columns]).start()
+
+                def run(ref, rows, columns):
+                    save(slot, ref.at[rows, columns]).start()
+                    send_final(slot, ref.at[rows, columns]).start()
+
+                on_late(k, lambda: each(k, spans, outs[:whole], late_index(k), run))
+                on_pre(k, lambda: each(k, pre_spans, outs[whole:], k // 3, run))
 
         stage(t, begin)
         stage(t - lag, add_core)
@@ -435,17 +511,20 @@
         stage(t - 6 * lag, finish)
 
 
-def sum_grads(grads, high=48, lag=2, slots=4):
-    shapes = [grad.shape for grad in grads]
-    spans, total = sum_plan(shapes, high)
+def sum_grads(grads, pres, high=48, lag=2, slots=4):
+    shapes = [(grad.shape[0] // 8, grad.shape[1]) for grad in grads]
+    pre_shapes = [grad.shape for grad in pres]
+    spans, late = sum_plan(shapes, high)
+    pre_spans, pre = sum_plan(pre_shapes, high)
     half = WIDE // 2
     anywhere = pl.BlockSpec(memory_space=pl.ANY)
     blocks = [grad.reshape(4, 2, grad.shape[0] // 8, grad.shape[1]) for grad in grads]
+    shapes = shapes + pre_shapes
     return pl.pallas_call(
-        partial(sum_kernel, spans, total, high, lag, slots),
-        in_specs=[anywhere] * len(grads),
-        out_specs=[anywhere] * len(grads),
-        out_shape=[jax.ShapeDtypeStruct((rows // 8, columns), BF) for rows, columns in shapes],
+        partial(sum_kernel, spans, pre_spans, late, pre, high, lag, slots),
+        in_specs=[anywhere] * len(shapes),
+        out_specs=[anywhere] * len(shapes),
+        out_shape=[jax.ShapeDtypeStruct(shape, BF) for shape in shapes],
         scratch_shapes=[
             pltpu.VMEM((slots, 4, high, WIDE), BF),
             pltpu.VMEM((slots, 4, high, WIDE), BF),
@@ -461,12 +540,13 @@
             pltpu.VMEM((slots, high, WIDE), BF),
             pltpu.VMEM((slots, high, WIDE), BF),
             pltpu.VMEM((slots, high, WIDE), BF),
-            pltpu.SemaphoreType.DMA((18, slots)),
+            pltpu.VMEM((slots, high, WIDE), BF),
+            pltpu.SemaphoreType.DMA((20, slots)),
             pltpu.SemaphoreType.REGULAR((8,)),
         ],
         compiler_params=pltpu.CompilerParams(collective_id=1, has_side_effects=True),
         name="sum_grads",
-    )(*blocks)
+    )(*blocks, *pres)
 
 
 def heads_first(weight, parts):
@@ -481,73 +561,90 @@
     return split.transpose(0, 2, 1, 3).reshape(rows, 3 * WIDE)
 
 
-def gather_weights(big, small):
-    copies = [piece.astype(BF) for piece in big]
-    sizes = [piece.size for piece in small]
-    flat = jnp.concatenate([piece.reshape(-1) for piece in small]).astype(BF)
-    columns = copies[0].shape[1]
-    high = -(-flat.size // columns)
+def flat_small(small):
+    return jnp.concatenate([piece.T.reshape(-1) for piece in small])
+
+
+def gather_first(weight, shift):
+    rows, columns = weight.shape
+    tail = jnp.pad(shift[None], ((0, 7), (0, columns - shift.size)))
+    both = jnp.concatenate([weight.astype(BF), tail.astype(BF)], axis=0)
+    full = lax.all_gather(both, "dp", axis=0)
+    return full[:, :rows].reshape(-1, columns), full[:, rows, : shift.size].reshape(-1).astype(F32)
+
+
+def gather_middle(weights, small):
+    pieces = []
+    for weight in weights:
+        low = weight.astype(BF)
+        pieces += [low[:, start : start + WIDE] for start in range(0, low.shape[1], WIDE)]
+    flat = flat_small(small).astype(BF)
+    high = -(-flat.size // WIDE)
     high = -(-high // 8) * 8
-    flat = jnp.pad(flat, (0, high * columns - flat.size)).reshape(high, columns)
-    rows = copies[-1].shape[0]
-    copies[-1] = jnp.concatenate([copies[-1], flat], axis=0)
-    full = [lax.all_gather(piece, "dp", axis=0) for piece in copies]
-    last = full[-1]
-    full[-1] = last[:, :rows]
-    full = [piece.reshape(-1, piece.shape[-1]) for piece in full]
-    table = last[:, rows:].reshape(last.shape[0], -1)
-    vectors = []
-    start = 0
-    for piece, size in zip(small, sizes):
-        part = table[:, start : start + size]
-        vectors.append(part.reshape((-1,) + piece.shape[1:]).astype(F32))
-        start += size
-    return full, vectors
+    pieces.append(jnp.pad(flat, (0, high * WIDE - flat.size)).reshape(high, WIDE))
+    full = lax.all_gather(jnp.concatenate(pieces, axis=0), "dp", axis=0)
+    groups = full.shape[0]
+    outs, at = [], 0
+    for weight in weights:
+        rows, columns = weight.shape
+        blocks = columns // WIDE
+        part = full[:, at : at + blocks * rows].reshape(groups, blocks, rows, WIDE)
+        outs.append(part.transpose(0, 2, 1, 3).reshape(groups * rows, columns))
+        at += blocks * rows
+    table = full[:, at:].reshape(groups, -1).astype(F32)
+    vectors, at = [], 0
+    for piece in small:
+        part = table[:, at : at + piece.size]
+        if piece.ndim == 2:
+            rows, columns = piece.shape
+            part = part.reshape(groups, columns, rows).transpose(1, 0, 2)
+            vectors.append(part.reshape(columns, groups * rows))
+        else:
+            vectors.append(part.reshape(-1))
+        at += piece.size
+    return outs, vectors
 
 
 def pack_small(small, groups, multiple):
-    flat = jnp.concatenate([piece.reshape(groups, -1) for piece in small], axis=1)
+    pieces = []
+    for piece in small:
+        columns = piece if isinstance(piece, list) else [piece]
+        pieces += [column.reshape(groups, -1) for column in columns]
+    flat = jnp.concatenate(pieces, axis=1)
     high = -(-flat.shape[1] // WIDE)
     high = -(-high // multiple) * multiple
-    flat = jnp.pad(flat, ((0, 0), (0, high * WIDE - flat.shape[1])))
-    return flat.reshape(groups * high, WIDE).astype(BF)
-
-
-def sum_grads_plain(grads):
-    groups = lax.axis_size("dp")
-    blocks = []
-    for grad in grads:
-        rows, columns = grad.shape
-        for start in range(0, columns, WIDE):
-            blocks.append(grad[:, start : start + WIDE].reshape(groups, rows // groups, WIDE))
-    packed = jnp.concatenate(blocks, axis=1)
-    mine = lax.psum_scatter(packed, "dp", scatter_dimension=0, tiled=False)
-    mine = lax.psum(mine, "seq")
-    outs, at = [], 0
-    for grad in grads:
-        rows, columns = grad.shape[0] // groups, grad.shape[1]
-        parts = []
-        for _ in range(columns // WIDE):
-            parts.append(mine[at : at + rows])
-            at += rows
-        outs.append(jnp.concatenate(parts, axis=1))
-    return outs
-
-
-def reduce_grads(big, small):
+    flat = jnp.pad(flat.astype(BF), ((0, 0), (0, high * WIDE - flat.shape[1])))
+    return flat.reshape(groups * high, WIDE)
+
+
+def sum_grads_plain(grads, pres):
+    outs = [lax.psum_scatter(grad, "dp", scatter_dimension=0, tiled=True) for grad in grads]
+    return [lax.psum(part, "seq") for part in outs + list(pres)]
+
+
+def reduce_grads(big, pres, small):
     groups = lax.axis_size("dp")
     ours = groups == 8 and lax.axis_size("seq") == 4
     grads = [grad.astype(BF) for grad in big] + [pack_small(small, groups, 48)]
-    outs = sum_grads(grads) if ours else sum_grads_plain(grads)
-    outs = [piece.astype(F32) for piece in outs]
-    tail = outs.pop().reshape(-1)
-    start = 0
+    outs = sum_grads(grads, pres) if ours else sum_grads_plain(grads, pres)
+    tail = outs[len(big)]
+    sizes = []
     for piece in small:
-        size = piece.size // groups
-        shape = (piece.shape[0] // groups,) + piece.shape[1:]
-        outs.append(tail[start : start + size].reshape(shape))
-        start += size
-    return outs
+        columns = piece if isinstance(piece, list) else [piece]
+        sizes.append((len(columns), columns[0].size // groups, isinstance(piece, list)))
+    used = -(-sum(many * size for many, size, _ in sizes) // WIDE)
+    tail = tail[:used].astype(F32).reshape(-1)
+    vectors, at = [], 0
+    for many, size, matrix in sizes:
+        part = tail[at : at + many * size]
+        vectors.append(part.reshape(many, size).T if matrix else part)
+        at += many * size
+    bigs = [piece.astype(F32) for piece in outs[: len(big)]]
+    return bigs, [piece.astype(F32) for piece in outs[len(big) + 1 :]], vectors
+
+
+def scatter_sum(grad):
+    return lax.psum_scatter(grad.astype(BF), "dp", scatter_dimension=0, tiled=True)
 
 
 def body(
@@ -582,11 +679,13 @@
     masks = perm[:, 0]
     place = lax.axis_index("dp")
     own_lengths = lax.dynamic_slice(lengths, (place * seqs,), (seqs,))
-    big = (heads_first(w_qkv, parts), gru_x, w_out, w_in, w_back, blend_w, conv_w, gru_h)
-    small = (b_qv, b_in, gru_bias, conv_b, norm_gain, norm_bias, row_bias)
-    full, vectors = gather_weights(big, small)
-    w_qkv, gru_x, w_out, w_in, w_back, blend_w, conv_w, gru_h = full
-    b_qv, b_in, gru_bias, conv_b, norm_gain, norm_bias, row_bias = vectors
+    w_qkv, b_qv = gather_first(heads_first(w_qkv, parts), b_qv)
+    middle = (gru_x, gru_h, w_out, w_in, w_back, blend_w)
+    small = (b_in, gru_bias, conv_b, norm_gain, norm_bias, row_bias)
+    middle, small = gather_middle(middle, small)
+    gru_x, gru_h, w_out, w_in, w_back, blend_w = middle
+    b_in, gru_bias, conv_b, norm_gain, norm_bias, row_bias = small
+    conv_w = lax.all_gather(conv_w.astype(BF), "dp", axis=0, tiled=True)
 
     flat_tokens = tokens.reshape(rows, width)
     bias = jnp.concatenate([b_qv[:width], jnp.zeros((width,), F32), b_qv[width:]])
@@ -600,7 +699,7 @@
 
     counts = char_counts.reshape(rows, 1)
     flat_chars = chars.transpose(2, 0, 1, 3).reshape(NCHAR * rows, width)
-    gates = (dot_plain(flat_chars, gru_x) + gru_bias[:, 0]).reshape(NCHAR, rows, 2 * three)
+    gates = (dot_plain(flat_chars, gru_x) + gru_bias[0]).reshape(NCHAR, rows, 2 * three)
     sides = []
     for side in range(2):
         columns = slice(side * three, (side + 1) * three)
@@ -610,7 +709,7 @@
             position = order if side == 0 else NCHAR - 1 - order
             live = position < counts
             low = state.astype(BF)
-            recur = dot_plain(low, gru_h[:, columns]) + gru_bias[columns, 1]
+            recur = dot_plain(low, gru_h[:, columns]) + gru_bias[1, columns]
             steps.append((position, live, low, recur, state))
             state = gru_cell(live, gates[position, :, columns], recur, state)
         sides.append((state, steps))
@@ -618,17 +717,17 @@
 
     cots = jnp.concatenate([token_cot, char_cot], axis=-1)
     cots = relocate(masks, cots, (project, context, context))
-    summed_first = flat_tokens.astype(F32) + dot_plain(context, w_out) + row_bias[:, 0]
-    hidden1 = norm_rows(summed_first, norm_gain[:, 0], norm_bias[:, 0])
+    summed_first = flat_tokens.astype(F32) + dot_plain(context, w_out) + row_bias[0]
+    hidden1 = norm_rows(summed_first, norm_gain[0], norm_bias[0])
     hidden1_low = hidden1.astype(BF)
     inner = dot_plain(hidden1_low, w_in) + b_in
     activated = gelu_exact(inner).astype(BF)
-    summed_second = hidden1 + dot_plain(activated, w_back) + row_bias[:, 1]
-    hidden2 = norm_rows(summed_second, norm_gain[:, 1], norm_bias[:, 1])
+    summed_second = hidden1 + dot_plain(activated, w_back) + row_bias[1]
+    hidden2 = norm_rows(summed_second, norm_gain[1], norm_bias[1])
     hidden2_low = hidden2.astype(BF)
     char_low = char_state.astype(BF)
-    token_side = dot_plain(hidden2_low, blend_w[:, :width]) + row_bias[:, 2]
-    char_side = dot_plain(char_low, blend_w[:, width:]) + row_bias[:, 3]
+    token_side = dot_plain(hidden2_low, blend_w[:, :width]) + row_bias[2]
+    char_side = dot_plain(char_low, blend_w[:, width:]) + row_bias[3]
     joined = jnp.concatenate([token_side, char_side], axis=-1).astype(BF)
     joined = joined.reshape(seqs, local, 2 * width)
     taps = shifted(joined, *edges(joined))
@@ -637,18 +736,23 @@
     lifted = gelu_exact(mixed)
     token_pre = hidden2 + lifted[:, :width]
     char_pre = char_state + lifted[:, width:]
-    token_out = norm_rows(token_pre, norm_gain[:, 2], norm_bias[:, 2]).astype(BF)
-    char_out = norm_rows(char_pre, norm_gain[:, 3], norm_bias[:, 3]).astype(BF)
+    token_out = norm_rows(token_pre, norm_gain[2], norm_bias[2]).astype(BF)
+    char_out = norm_rows(char_pre, norm_gain[3], norm_bias[3]).astype(BF)
     outs = jnp.concatenate([token_out, char_out], axis=-1).reshape(seqs, local, 2 * width)
 
     flat_cots = cots.reshape(rows, 2 * width).astype(F32)
     d_token_pre, gain_token, shift_token = norm_back(
-        token_pre, norm_gain[:, 2], flat_cots[:, :width]
+        token_pre, norm_gain[2], flat_cots[:, :width]
     )
-    d_char_pre, gain_char, shift_char = norm_back(char_pre, norm_gain[:, 3], flat_cots[:, width:])
+    d_char_pre, gain_char, shift_char = norm_back(char_pre, norm_gain[3], flat_cots[:, width:])
     d_mixed = jnp.concatenate([d_token_pre, d_char_pre], axis=-1) * gelu_slope(mixed)
     d_mixed = d_mixed.astype(BF)
-    grad_conv = dot_left(stacked, d_mixed)
+    grad_conv = dot_left(stacked, d_mixed).astype(BF)
+    grad_conv, d_mixed = lax.optimization_barrier((grad_conv, d_mixed))
+    sum_conv = scatter_sum(grad_conv)
+    other, kept, moving = relocate_step(masks, outs, 0)
+    other, kept, d_mixed = lax.optimization_barrier((other, kept, d_mixed))
+    outs = jnp.where(moving, other, kept)
     beside = d_mixed.reshape(seqs, local, 2 * width)
     before, same, after = shifted(beside, *edges(beside))
     taps_w = conv_w.reshape(3, 2 * width, 2 * width)
@@ -659,21 +763,33 @@
     grad_blend = jnp.concatenate(
         [dot_left(hidden2_low, d_token_side), dot_left(char_low, d_char_side)], axis=-1
     )
+    grad_blend, d_token_side, d_char_side = lax.optimization_barrier(
+        (grad_blend.astype(BF), d_token_side, d_char_side)
+    )
+    sum_blend = scatter_sum(grad_blend)
     d_hidden2 = d_token_pre + dot_right(d_token_side, blend_w[:, :width])
     d_char_state = d_char_pre + dot_right(d_char_side, blend_w[:, width:])
 
-    d_second, gain_second, shift_second = norm_back(summed_second, norm_gain[:, 1], d_hidden2)
+    d_second, gain_second, shift_second = norm_back(summed_second, norm_gain[1], d_hidden2)
     d_branch = d_second.astype(BF)
-    grad_back = dot_left(activated, d_branch)
+    grad_back = dot_left(activated, d_branch).astype(BF)
+    grad_back, d_branch = lax.optimization_barrier((grad_back, d_branch))
+    sum_back = scatter_sum(grad_back)
     d_inner = (dot_right(d_branch, w_back) * gelu_slope(inner)).astype(BF)
     grad_in = dot_left(hidden1_low, d_inner)
     d_hidden1 = d_second + dot_right(d_inner, w_in)
-    d_first, gain_first, shift_first = norm_back(summed_first, norm_gain[:, 0], d_hidden1)
+    d_first, gain_first, shift_first = norm_back(summed_first, norm_gain[0], d_hidden1)
     d_attend = d_first.astype(BF)
+    other, kept, moving = relocate_step(masks, outs, 1)
+    other, kept, d_attend = lax.optimization_barrier((other, kept, d_attend))
+    outs = jnp.where(moving, other, kept)
     grad_out = dot_left(context, d_attend)
     d_context = dot_right(d_attend, w_out).astype(BF)
     d_context = d_context.reshape(seqs, local, parts, per * HEAD).transpose(2, 0, 1, 3)
-    d_project = exchange(attention_backward(qkv, exchange(d_context), own_lengths, per))
+    d_project = attention_backward(qkv, exchange(d_context), own_lengths, per)
+    sum_conv, d_char_state, d_project = lax.optimization_barrier((sum_conv, d_char_state, d_project))
+    d_project = exchange(d_project)
+    sum_conv = line_sum(sum_conv, 0)
     d_project = d_project.transpose(1, 2, 0, 3).reshape(rows, 3 * width)
 
     d_gates = [[None, None] for _ in range(NCHAR)]
@@ -693,44 +809,51 @@
             d_state = d_keep + dot_right(d_recur, gru_h[:, columns])
             d_gates[position][side] = d_gate.astype(BF)
         lows, recurs = jnp.concatenate(lows, axis=0), jnp.concatenate(recurs, axis=0)
+        if side == 0:
+            sum_conv, recurs, d_char_state = lax.optimization_barrier(
+                (sum_conv, recurs, d_char_state)
+            )
+            sum_conv = line_sum(sum_conv, 1)
         grad_side.append(dot_left(lows, recurs))
         bias_side.append(column_sum(recurs))
     d_gates = jnp.concatenate([jnp.concatenate(pair, axis=-1) for pair in d_gates], axis=0)
+    sum_conv, d_gates = lax.optimization_barrier((sum_conv, d_gates))
     grad_gru_x = dot_left(flat_chars, d_gates)
     chars_back = dot_right(d_gates, gru_x).astype(BF)
     chars_back = chars_back.reshape(NCHAR, seqs, local, width).transpose(1, 2, 0, 3)
     grad_gru_h = jnp.concatenate(grad_side, axis=-1)
-    grad_gru_bias = jnp.stack([column_sum(d_gates), jnp.concatenate(bias_side)], axis=-1)
-
-    outs = relocate(masks, outs, (d_joined, d_inner, d_context))
+    grad_gru_bias = [column_sum(d_gates), jnp.concatenate(bias_side)]
+
     grad_qkv = dot_left(flat_tokens, d_project)
     sums = heads_last(column_sum(d_project)[None], parts)[0]
     grad_b_qv = jnp.concatenate([sums[:width], sums[2 * width :]])
     tokens_back = (d_first + dot_right(d_project, w_qkv)).astype(BF)
-    grad_gain = jnp.stack([gain_first, gain_second, gain_token, gain_char], axis=-1)
-    grad_shift = jnp.stack([shift_first, shift_second, shift_token, shift_char], axis=-1)
-    grad_rows = jnp.stack(
+    big = (grad_in, grad_qkv, grad_gru_x, grad_gru_h, grad_out)
+    small = (
+        grad_b_qv,
+        column_sum(d_inner),
+        grad_gru_bias,
+        column_sum(d_mixed),
+        [gain_first, gain_second, gain_token, gain_char],
+        [shift_first, shift_second, shift_token, shift_char],
         [
             column_sum(d_attend),
             column_sum(d_branch),
             column_sum(d_token_side),
             column_sum(d_char_side),
         ],
-        axis=-1,
     )
-    big = (grad_qkv, grad_gru_x, grad_out, grad_in, grad_back, grad_blend, grad_conv, grad_gru_h)
-    small = (
-        grad_b_qv,
-        column_sum(d_inner),
-        grad_gru_bias,
-        column_sum(d_mixed),
-        grad_gain,
-        grad_shift,
-        grad_rows,
-    )
-    summed = reduce_grads(big, small)
-    g_qkv, g_gru_x, g_out, g_in, g_back, g_blend, g_conv, g_gru_h = summed[:8]
-    g_b_qv, g_b_in, g_gru_bias, g_conv_b, g_gain, g_shift, g_rows = summed[8:]
+    big, early, small = reduce_grads(big, (sum_back, sum_blend), small)
+    other, kept, moving = relocate_step(masks, outs, 2)
+    for bit in range(3, lax.axis_size("dp").bit_length() - 1):
+        outs = jnp.where(moving, other, kept)
+        other, kept, moving = relocate_step(masks, outs, bit)
+    other, kept, _ = lax.optimization_barrier((other, kept, big[-1]))
+    outs = jnp.where(moving, other, kept)
+    g_in, g_qkv, g_gru_x, g_gru_h, g_out = big
+    g_back, g_blend = early
+    g_conv = line_sum(sum_conv, 2).astype(F32)
+    g_b_qv, g_b_in, g_gru_bias, g_conv_b, g_gain, g_shift, g_rows = small
     return (
         outs[..., :width],
         outs[..., width:],

time: 904 us -> 914 us (1.011)
  Pallas kernels: 224 us -> 159 us
  local copies, waits for them, and re-layouts: 145 us -> 169 us
  other arithmetic: 121 us -> 144 us
  blocking collectives: 0 us -> 22.1 us
  matrix products: 188 us -> 172 us
  waiting for transfers between devices: 168 us -> 184 us
    all_gather x8 -> x3, waiting for transfers between devices: 127 us -> 32.3 us  [the longest x1 32.3 us: gather_first(): full = lax.all_gather(both, 'dp', axis=0)]
    ppermute x6 -> x9, waiting for transfers between devices: 22.2 us -> 100 us  [the longest x3 51.7 us: line_sum(): other = lax.ppermute(value, 'seq', LINE[step])]
    pallas_call x1, Pallas kernels: 167 us -> 103 us  [sum_grads(): pl.pallas_call(partial(sum_kernel, spans, pre_spans, late, pre, high, lag...]
    all_to_all x4 -> x3, waiting for transfers between devices: 15.6 us -> 50.6 us  [exchange(): return lax.all_to_all(blocks, 'seq', split_axis=0, concat_axis=0)]
    all_to_all x0 -> x1, blocking collectives: none -> 22.1 us  [exchange(): return lax.all_to_all(blocks, 'seq', split_axis=0, concat_axis=0)]
    unnamed x389 -> x425, local copies, waits for them, and re-layouts: 38 us -> 55 us
    reshape x12 -> x28, local copies, waits for them, and re-layouts: 2.8 us -> 18.9 us  [the longest x15 8.6 us: pack_small(): pieces += [column.reshape(groups, -1) for column in columns]]
    transpose x0 -> x6, local copies, waits for them, and re-layouts: none -> 14.9 us  [the longest x4 14.3 us: gather_middle(): outs.append(part.transpose(0, 2, 1, 3).reshape(groups * rows, columns))]
  transfers between devices with their start and end apart: 22 -> 22, of which waited for: 11 -> 8; matrix products, arithmetic and copies ran while one was open for 37% -> 44% of each run, Pallas kernels for 6% -> 18%
where the time goes in v3:
time: 914 us; the launch traced here: 904 us
  waiting for transfers between devices  184 us (20%)
  matrix products  172 us (19%)
  local copies, waits for them, and re-layouts  169 us (18%)
  Pallas kernels  159 us (17%)
  other arithmetic  144 us (16%)
  starting transfers between devices  36.2 us (4%)
  blocking collectives  22.1 us (2%)
  between operations  17.2 us (2%)
    pallas_call x1, Pallas kernels, sum_grads(): pl.pallas_call(partial(sum_kernel, spans, pre_spans, late, pre, high, lag...  103 us
    dot_general x16, matrix products, dot_plain(): return jnp.dot(left, right, preferred_element_type=F32)  70.8 us
    unnamed x425, local copies, waits for them, and re-layouts  55 us
    dot_general x16, matrix products, dot_right(): lax.dot_general(left, right, (((1,), (1,)), ((), ())), preferred_element_...  53.5 us
    ppermute x3, waiting for transfers between devices, line_sum(): other = lax.ppermute(value, 'seq', LINE[step])  51.7 us
    all_to_all x3, waiting for transfers between devices, exchange(): return lax.all_to_all(blocks, 'seq', split_axis=0, concat_axis=0)  50.6 us
    ppermute x6, waiting for transfers between devices, relocate_step(): other = lax.ppermute(value, 'dp', pairs)  48.3 us
    dot_general x10, matrix products, dot_left(): lax.dot_general(left, right, (((0,), (0,)), ((), ())), preferred_element_...  47.3 us
  transfers between devices with their start and end apart: 22, of which 8 were waited for; matrix products, arithmetic and copies ran while one was open for 44% of the time, Pallas kernels for 18%

profile of v3, /device:TPU:0, one launch (start us, length us, event | category | flops | bytes accessed | tf_op | source)
XLA Modules:
  0.0 903.9 jit_solution(5774561657671527308)
XLA Ops:
  17.6 32.3 %all-gather.8.cloned.1.call-done = bf16[832,2304]{1,0:T(8,128)(2,1)} async-done(((bf16[104,2304]{1,0:T(8,128)(2,1)}), bf16[832,2304]{1,0:T(8,128)(2,1)}) %all-gather.8.cloned.1.call-update) | async-done | bytes 3833872 | tf_op jit(solution)/shard_map/all_gather | solution.py:572
  85.4 42.0 %all-to-all-done = bf16[4,2,256,576]{2,3,1,0:T(8,128)(2,1)S(1)} async-done(((bf16[4,2,256,576]{2,3,1,0:T(8,128)(2,1)}), bf16[4,2,256,576]{2,3,1,0:T(8,128)(2,1)S(1)}, u32[]{:S(2)}, u32[]{:S(2)}) %all-to-all-start) | async-done | bytes 2359328 | tf_op jit(solution)/shard_map/all_to_all | solution.py:176
  129.9 19.7 %attend_forward.1 = bf16[4,2,256,192]{3,2,1,0:T(8,128)(2,1)} custom-call(s32[2]{0:T(128)} %dynamic_slice.3.len_ref, bf16[4,2,256,576]{3,2,1,0:T(8,128)(2,1)} %copy.110.qkv_ref), custom_call_target="tpu_custom_call" | custom-call | tf_op jit(solution)/shard_map/attend_forward/pallas_call | solution.py:98
  151.1 22.1 %all_to_all.20 = bf16[4,2,256,192]{2,3,1,0:T(8,128)(2,1)S(1)} all-to-all(bf16[4,2,256,192]{2,3,1,0:T(8,128)(2,1)S(1)} %copy.111), channel_id=1, replica_groups=mesh['dp'=8,'seq'=4] {'seq'}, dimensions={0} | all-to-all | bytes 1572864 | tf_op jit(solution)/shard_map/all_to_all | solution.py:176
  185.0 46.1 %collective-permute-done.5 = bf16[2,256,1536]{2,1,0:T(8,128)(2,1)S(1)} collective-permute-done((bf16[2,256,1536]{2,1,0:T(8,128)(2,1)S(1)}, bf16[2,256,1536]{2,1,0:T(8,128)(2,1)S(1)}, u32[]{:S(2)}, u32[]{:S(2)}) %collective-permute-start.5) | collective-permute-done | bytes 1572896 | tf_op jit(solution)/shard_map/ppermute | solution.py:183
  257.4 6.8 fusion.299
  271.2 6.9 copy.115
  278.0 8.2 reshape.483
  289.2 18.0 %fusion.2 = (bf16[512,3072]{1,0:T(8,128)(2,1)S(1)}, f32[512,3072]{1,0:T(8,128)}) fusion(f32[3072]{0:T(1024)S(1)} %add.585, bf16[768,3072]{1,0:T(8,128)(2,1)S(1)} %bitcast.227, f32[512,768]{1,0:T(8,128)S(1)} %get-tuple-element.256, f32[768]{0:T(1024)S(1)} %add.582, f32[768]{0:T(1024)S(1)} %mul.649, f32[512]{0:T(512)S(1)} %add_rsqrt_fusion.3, ...), kind=kOutput, calls=%fused_computation.7 | convolution fusion | flops 2521694208 | bytes 15751168 | tf_op jit(solution)/shard_map/dot_general | solution.py:19
  315.6 10.9 %convolution_add_fusion = f32[2304,2048]{0,1:T(8,128)} fusion(bf16[768,2304]{0,1:T(8,128)(2,1)S(1)} %copy-done.52, bf16[2048,768]{1,0:T(8,128)(2,1)S(1)} %bitcast.244, f32[2304]{0:T(1024)S(1)} %copy-done.143), kind=kOutput, calls=%fused_computation.1 | convolution fusion | flops 7252475904 | bytes 25568256 | tf_op jit(solution)/shard_map/dot_general | solution.py:19
  326.5 9.3 %slice_bitcast_fusion.7 = (f32[512,1152]{1,0:T(8,128)S(1)}, f32[512,1152]{1,0:T(8,128)S(1)}, f32[512,1152]{1,0:T(8,128)S(1)}, f32[512,1152]{1,0:T(8,128)S(1)}, f...) fusion(f32[4,512,2304]{2,1,0:T(8,128)} %bitcast.206), kind=kLoop, calls=%fused_computation.148 | loop fusion | bytes 37748736 | tf_op jit(solution)/shard_map/squeeze | solution.py:714
  335.8 5.2 fusion.283
  379.2 20.2 %fusion.39 = (f32[512,1536]{1,0:T(8,128)S(1)}, f32[512,1536]{1,0:T(8,128)S(1)}) fusion(f32[1536]{0:T(1024)S(1)} %add.666, bf16[4608,1536]{1,0:T(8,128)(2,1)} %all-gather.6.cloned.1.call-done, bf16[512,1536]{1,0:T(8,128)(2,1)} %bitcast.258, bf16[512,768]{1,0:T(8,128)(2,1)} %copy-done.64, bf16[512,768]{1,0:T(8,128)(2,1)} %copy-done.66, ...), kind=kOutput, calls=%fused_computation.67 | convolution fusion | flops 7317749760 | bytes 25171968 | tf_op jit(solution)/shard_map/dot_general | solution.py:19
  409.7 12.5 %convolution_convert_fusion = bf16[4608,1536]{1,0:T(8,128)(2,1)} fusion(bf16[512,1536]{1,0:T(8,128)(2,1)S(1)} %fusion.45, bf16[512,1536]{1,0:T(8,128)(2,1)} %bitcast.259, bf16[512,768]{1,0:T(8,128)(2,1)S(1)} %copy-done.65, bf16[512,768]{1,0:T(8,128)(2,1)S(1)} %copy-done.67, bf16[512,1536]{1,0:T(8,128)(2,1)S(1)} %bitcast.257), kind=kOutput, calls=%fused_computation | convolution fusion | flops 7273709568 | bytes 20447232 | tf_op jit(solution)/shard_map/dot_general | solution.py:23
  467.7 7.5 fusion.309
  476.8 6.6 multiply_reduce_fusion.3
  518.2 8.7 all-to-all-done.2
  528.2 37.0 %attend_backward.1 = bf16[4,2,256,576]{3,2,1,0:T(8,128)(2,1)} custom-call(s32[2]{0:T(128)} %dynamic_slice.3.len_ref, bf16[4,2,256,576]{3,2,1,0:T(8,128)(2,1)} %copy.110.qkv_ref, bf16[4,2,256,192]{3,2,1,0:T(8,128)(2,1)} %copy.124.grad_ref), custom_call_target="tpu_custom_call" | custom-call | tf_op jit(solution)/shard_map/attend_backward/pallas_call | solution.py:155
  597.3 51.7 %collective-permute-done.10 = bf16[576,1536]{1,0:T(8,128)(2,1)S(1)} collective-permute-done((bf16[576,1536]{1,0:T(8,128)(2,1)S(1)}, bf16[576,1536]{1,0:T(8,128)(2,1)S(1)}, u32[]{:S(2)}, u32[]{:S(2)}) %collective-permute-start.10) | collective-permute-done | bytes 1769504 | tf_op jit(solution)/shard_map/ppermute | solution.py:213
  673.4 36.6 %maximum_maximum_fusion = bf16[2048,2304]{1,0:T(8,128)(2,1)} fusion(bf16[512,1152]{1,0:T(8,128)(2,1)S(1)} %fusion.73, bf16[512,1152]{1,0:T(8,128)(2,1)S(1)} %get-tuple-element.225, bf16[512,1152]{1,0:T(8,128)(2,1)S(1)} %fusion.71, bf16[512,1152]{1,0:T(8,128)(2,1)S(1)} %get-tuple-element.223, bf16[512,1152]{1,0:T(8,128)(2,1)S(1)} %fusion.69, ...), kind=kLoop, calls=%fused_computation.4 | loop fusion | flops 75497472 | bytes 18874368 | tf_op jit(solution)/shard_map/concatenate | solution.py:819
  743.0 10.1 %convolution_convert_fusion.1 = bf16[2304,768]{0,1:T(8,128)(2,1)} fusion(bf16[2048,2304]{1,0:T(8,128)(2,1)S(1)} %bitcast.188, bf16[2048,768]{1,0:T(8,128)(2,1)S(1)} %bitcast.245), kind=kOutput, calls=%fused_computation.29 | convolution fusion | flops 7249526784 | bytes 16121856 | tf_op jit(solution)/shard_map/dot_general | solution.py:23
  753.2 102.8 %sum_grads.1 = (bf16[96,3072]{1,0:T(8,128)(2,1)}, bf16[96,2304]{1,0:T(8,128)(2,1)}, bf16[96,2304]{1,0:T(8,128)(2,1)}, bf16[48,2304]{1,0:T(8,128)(2,1)}, bf16[96,...) custom-call(bf16[4,2,96,3072]{3,2,1,0:T(8,128)(2,1)} %bitcast.229, ...), custom_call_target="tpu_custom_call" | custom-call | tf_op jit(solution)/shard_map/sum_grads/pallas_call | solution.py:523
  857.3 11.1 %convolution_convert_fusion.5 = bf16[2048,768]{1,0:T(8,128)(2,1)} fusion(bf16[2048,2304]{1,0:T(8,128)(2,1)} %maximum_maximum_fusion, bf16[768,2304]{0,1:T(8,128)(2,1)S(1)} %copy-done.53), kind=kOutput, calls=%fused_computation.62 | convolution fusion | flops 7249330176 | bytes 16121856 | tf_op jit(solution)/shard_map/dot_general | solution.py:27
  869.8 6.1 copy.148
  (728 shorter events, 348.5 us)
Async XLA Ops:
  7.2 42.7 %all-gather.8.cloned.1.call-start = ((), (), s32[]{:S(2)}) async-start(), calls=%async_computation.11 | async-start | bytes 4313088 | tf_op jit(solution)/shard_map/all_gather | solution.py:572
  12.0 221.6 %all-gather.10.cloned.1.call-start = ((), (), s32[]{:S(2)}) async-start(), calls=%async_computation.12 | async-start | bytes 20680704 | tf_op jit(solution)/shard_map/all_gather | solution.py:585
  68.4 59.0 %all-to-all-start = ((bf16[4,2,256,576]{2,3,1,0:T(8,128)(2,1)}), bf16[4,2,256,576]{2,3,1,0:T(8,128)(2,1)S(1)}, u32[]{:S(2)}, u32[]{:S(2)}) async-start(bf16[4,2,256,576]{2,3,1,0:T(8,128)(2,1)} %copy.109), calls=%async_computation | async-start | bytes 4718592 | tf_op jit(solution)/shard_map/all_to_all | solution.py:176
  73.1 306.1 %all-gather.6.cloned.1.call-start = ((), (), s32[]{:S(2)}) async-start(), calls=%async_computation.7 | async-start | bytes 15925248 | tf_op jit(solution)/shard_map/all_gather | solution.py:688
  76.2 3.8 collective-permute-start.3
  79.8 485.4 %reduce-scatter.4.cloned.1.call-start = ((), (), s32[]{:S(2)}) async-start(), calls=%async_computation.8 | async-start | bytes 15925248 | tf_op jit(solution)/shard_map/reduce_scatter | solution.py:647
  80.0 151.2 %copy-start.158 = (pred[2]{0:T(512)(128)(4,1)}, pred[2]{0:T(512)(128)(4,1)S(1)}, u32[]{:S(2)}) copy-start(pred[2]{0:T(512)(128)(4,1)S(1)} %get-tuple-element.130) | copy-start | bytes 10
  83.3 91.8 %collective-permute-start.4 = (bf16[2,256,1536]{2,1,0:T(8,128)(2,1)}, bf16[2,256,1536]{2,1,0:T(8,128)(2,1)}, u32[]{:S(2)}, u32[]{:S(2)}) collective-permute-start(bf16[2,256,1536]{2,1,0:T(8,128)(2,1)} %broadcast_select_fusion.1), channel_id=1, source_target_pairs={{0,8},{4,12},{8,0},{12,4},{16,24},{20,28},{24,16},{28,20},{1,9},{5... | collective-permute-start | bytes 4718600 | tf_op jit(solution)/shard_map/ppermute | solution.py:183
  177.2 53.9 %collective-permute-start.5 = (bf16[2,256,1536]{2,1,0:T(8,128)(2,1)S(1)}, bf16[2,256,1536]{2,1,0:T(8,128)(2,1)S(1)}, u32[]{:S(2)}, u32[]{:S(2)}) collective-permute-start(bf16[2,256,1536]{2,1,0:T(8,128)(2,1)S(1)} %broadcast_select_fusion.3), channel_id=1, source_target_pairs={{0,16},{4,20},{8,24},{12,28},{16,0},{20,4},{24,8},{28,12},{1,17},{... | collective-permute-start | bytes 4718600 | tf_op jit(solution)/shard_map/ppermute | solution.py:183
  251.1 110.4 %copy-start = (bf16[48,8,3,768]{3,1,2,0:T(8,128)(2,1)}, bf16[48,8,3,768]{3,1,2,0:T(8,128)(2,1)S(1)}, u32[]{:S(2)}) copy-start(bf16[48,8,3,768]{3,1,2,0:T(8,128)(2,1)S(1)} %copy.142) | copy-start | bytes 5308420
  367.4 6.2 collective-permute-start
  372.4 5.6 collective-permute-start.1
  422.2 331.0 %reduce-scatter.8.cloned.1.call-start = ((), (), s32[]{:S(2)}) async-start(), calls=%async_computation.10 | async-start | bytes 2654208 | tf_op jit(solution)/shard_map/reduce_scatter | solution.py:647
  424.9 4.5 collective-permute-start.2
  430.3 16.4 %collective-permute-start.7 = (bf16[2,1,1536]{2,1,0:T(2,128)(2,1)S(1)}, bf16[2,1,1536]{2,1,0:T(2,128)(2,1)S(1)}, u32[]{:S(2)}, u32[]{:S(2)}) collective-permute-start(bf16[2,1,1536]{2,1,0:T(2,128)(2,1)S(1)} %get-tuple-element.231), channel_id=1, source_target_pairs={{1,0},{2,1},{3,2},{5,4},{6,5},{7,6},{9,8},{10,9},{11,10},{13,12},{... | collective-permute-start | bytes 18440 | tf_op jit(solution)/shard_map/ppermute | solution.py:203
  431.6 15.2 %collective-permute-start.8 = (bf16[2,1,1536]{2,1,0:T(2,128)(2,1)S(1)}, bf16[2,1,1536]{2,1,0:T(2,128)(2,1)S(1)}, u32[]{:S(2)}, u32[]{:S(2)}) collective-permute-start(bf16[2,1,1536]{2,1,0:T(2,128)(2,1)S(1)} %get-tuple-element.232), channel_id=1, source_target_pairs={{0,1},{1,2},{2,3},{4,5},{5,6},{6,7},{8,9},{9,10},{10,11},{12,13},{... | collective-permute-start | bytes 18440 | tf_op jit(solution)/shard_map/ppermute | solution.py:202
  440.3 57.9 %collective-permute-start.6 = (bf16[2,256,1536]{2,1,0:T(8,128)(2,1)}, bf16[2,256,1536]{2,1,0:T(8,128)(2,1)}, u32[]{:S(2)}, u32[]{:S(2)}) collective-permute-start(bf16[2,256,1536]{2,1,0:T(8,128)(2,1)} %broadcast_select_fusion), channel_id=1, source_target_pairs={{0,8},{4,12},{8,0},{12,4},{16,24},{20,28},{24,16},{28,20},{1,9},{5... | collective-permute-start | bytes 4718600 | tf_op jit(solution)/shard_map/ppermute | solution.py:183
  457.6 295.6 %reduce-scatter.6.cloned.1.call-start = ((), (), s32[]{:S(2)}) async-start(), calls=%async_computation.9 | async-start | bytes 5308416 | tf_op jit(solution)/shard_map/reduce_scatter | solution.py:647
  502.5 24.4 %all-to-all-start.2 = ((bf16[4,2,256,192]{2,3,1,0:T(8,128)(2,1)}), bf16[4,2,256,192]{2,3,1,0:T(8,128)(2,1)S(1)}, u32[]{:S(2)}, u32[]{:S(2)}) async-start(bf16[4,2,256,192]{2,3,1,0:T(8,128)(2,1)} %copy.122), calls=%async_computation.3 | async-start | bytes 1572864 | tf_op jit(solution)/shard_map/all_to_all | solution.py:176
  515.5 361.8 %collective-permute-start.9 = (bf16[2,256,1536]{2,1,0:T(8,128)(2,1)}, bf16[2,256,1536]{2,1,0:T(8,128)(2,1)}, u32[]{:S(2)}, u32[]{:S(2)}) collective-permute-start(bf16[2,256,1536]{2,1,0:T(8,128)(2,1)} %broadcast_select_fusion.2), channel_id=1, source_target_pairs={{0,16},{4,20},{8,24},{12,28},{16,0},{20,4},{24,8},{28,12},{1,17},{... | collective-permute-start | bytes 4718600 | tf_op jit(solution)/shard_map/ppermute | solution.py:183
  569.6 151.8 %all-to-all-start.3 = ((bf16[4,2,256,576]{2,3,1,0:T(8,128)(2,1)}), bf16[4,2,256,576]{2,3,1,0:T(8,128)(2,1)S(1)}, u32[]{:S(2)}, u32[]{:S(2)}) async-start(bf16[4,2,256,576]{2,3,1,0:T(8,128)(2,1)} %copy.125), calls=%async_computation.4 | async-start | bytes 4718592 | tf_op jit(solution)/shard_map/all_to_all | solution.py:176
  588.1 60.9 %collective-permute-start.10 = (bf16[576,1536]{1,0:T(8,128)(2,1)S(1)}, bf16[576,1536]{1,0:T(8,128)(2,1)S(1)}, u32[]{:S(2)}, u32[]{:S(2)}) collective-permute-start(bf16[576,1536]{1,0:T(8,128)(2,1)S(1)} %copy-done.85), channel_id=1, source_target_pairs={{0,1},{3,2},{4,5},{7,6},{8,9},{11,10},{12,13},{15,14},{16,17},{19,... | collective-permute-start | bytes 5308424 | tf_op jit(solution)/shard_map/ppermute | solution.py:213
  666.7 55.2 %collective-permute-start.11 = (bf16[576,1536]{1,0:T(8,128)(2,1)}, bf16[576,1536]{1,0:T(8,128)(2,1)}, u32[]{:S(2)}, u32[]{:S(2)}) collective-permute-start(bf16[576,1536]{1,0:T(8,128)(2,1)} %add.688), channel_id=1, source_target_pairs={{1,2},{2,1},{5,6},{6,5},{9,10},{10,9},{13,14},{14,13},{17,18},{18,... | collective-permute-start | bytes 5308424 | tf_op jit(solution)/shard_map/ppermute | solution.py:213
  732.1 161.3 %collective-permute-start.12 = (bf16[576,1536]{1,0:T(8,128)(2,1)}, bf16[576,1536]{1,0:T(8,128)(2,1)}, u32[]{:S(2)}, u32[]{:S(2)}) collective-permute-start(bf16[576,1536]{1,0:T(8,128)(2,1)} %add.696), channel_id=1, source_target_pairs={{1,0},{2,3},{5,4},{6,7},{9,8},{10,11},{13,12},{14,15},{17,16},{18,... | collective-permute-start | bytes 5308424 | tf_op jit(solution)/shard_map/ppermute | solution.py:213
  (199 other events, 1692.1 us)
Sparse Core Ops, SparseCore 0:
  12.1 37.7 all-gather.7
  52.4 121.3 all-gather.9
  175.6 97.6 all-gather.5
  422.3 140.2 reduce-scatter.3
  565.8 42.3 reduce-scatter.7
  611.5 53.7 reduce-scatter.5
